TPU v7x, 128 devices: a whole 4x4x4 slice. The times are simulated.
128 devices in a mesh: ctx: 16 (over z, x), head: 8 (over y, core).
Axes of the slice: x: 4, y: 4, z: 4, core: 2. Of those that a mesh axis runs over, the one named last changes fastest.
Arguments:
- values: bfloat16 [16384, 5120], P(('ctx', 'head')), may hold values from -6 to 6
- state_in: bfloat16 [16384, 128], P('ctx'), may hold values from -0.5 to 0.5
- state_out: bfloat16 [16384, 128], P('ctx'), may hold values from -6 to 6
- log_decay: float32 [16384, 80], P('ctx', 'head'), may hold values from -1 to 0
- level_class: int32 [16384], P('ctx'), may hold values from 0 to 31
- level_table: float32 [32, 9, 80], P(None, None, 'head'), may hold values from 0.2 to 2
- skip_gain: float32 [80], P('head'), may hold values from 0.5 to 2
- norm_gain: float32 [5120], P('head'), may hold values from 0.1 to 1.9
- out_weight: bfloat16 [5120, 2560], P('head', 'ctx'), may hold values from -0.078125 to 0.078125
Outputs:
- projected: bfloat16 [16384, 2560], P(('ctx', 'head'))
All inputs are finite; a program needn't handle non-finite values.
Results may differ from a plain program's by a relative error of at most 0.0049.
Values may be sent and summed in bfloat16 or wider, within the bound.
A program may use at most 128 MiB of HBM per device.

v0:
```python
import jax
import jax.numpy as jnp
from jax import lax
from jax.experimental import pallas as pl
from jax.experimental.pallas import tpu as pltpu
from jax.sharding import PartitionSpec as P

MESH = pl.DeviceIdType.MESH
PRECISE = lax.Precision.HIGHEST
EPSILON = 1e-05
F32 = jnp.float32
BF16 = jnp.bfloat16
LANES = 128
HEADS_DEV = 10
WIDTH = 64
FEATS = HEADS_DEV * WIDTH
STATE = 128
CHUNK = 128
CHUNKS = 8
OUTS = 2560
LIFT = 9

NT = (((1,), (1,)), ((), ()))
TN = (((0,), (0,)), ((), ()))
NN = (((1,), (0,)), ((), ()))


def iota(shape, axis):
    return lax.broadcasted_iota(jnp.int32, shape, axis)


def dot(a, b, dims=NN):
    return lax.dot_general(a, b, dims, preferred_element_type=F32)


def exact(a, b, dims=NN):
    return lax.dot_general(a, b, dims, precision=PRECISE, preferred_element_type=F32)


def split(value):
    high = value.astype(BF16)
    low = (value - high.astype(F32)).astype(BF16)
    return jnp.concatenate([high, low], axis=1)


def kernel(
    values,
    state_in,
    state_out,
    log_decay,
    level_class,
    level_table,
    skip_gain,
    norm_gain,
    weight,
    result,
    rows,
    entering,
    leaving,
    decay,
    classes,
    table,
    skip,
    gain,
    all_weight,
    expander,
    within,
    stretch,
    factors,
    totals,
    row_factors,
    mix_factors,
    pair_state,
    quad_state,
    half_state,
    output,
    ring_x,
    ring_z,
    buckets,
    normed_send,
    normed_all,
    own_sum,
    partial_send,
    partial_recv,
    local_sem,
    a_send,
    a_recv,
    w1_send,
    w1_recv,
    w2_send,
    w2_recv,
    wf_send,
    wf_recv,
    t_send,
    t_recv,
    x_send,
    x_recv,
    z_send,
    z_recv,
    n_send,
    n_recv,
    p_send,
    p_recv,
):
    ctx = lax.axis_index("ctx")
    head = lax.axis_index("head")
    x = lax.rem(ctx, 4)
    z = ctx // 4
    y = head // 2
    core = lax.rem(head, 2)
    partner = y * 2 + (1 - core)

    def copy(source, target, send, recv, device):
        return pltpu.make_async_remote_copy(
            src_ref=source,
            dst_ref=target,
            send_sem=send,
            recv_sem=recv,
            device_id=device,
            device_id_type=MESH,
        )

    loads = [
        pltpu.make_async_copy(source, target, local_sem.at[number])
        for number, (source, target) in enumerate(
            [
                (log_decay, decay),
                (level_class, classes),
                (level_table, table),
                (state_in, entering),
                (state_out, leaving),
                (skip_gain, skip),
                (norm_gain, gain),
            ]
        )
    ]
    for load in loads:
        load.start()
    own_lanes = pl.ds(pl.multiple_of(core * FEATS, LANES), FEATS)
    other_lanes = pl.ds(pl.multiple_of((1 - core) * FEATS, LANES), FEATS)
    own_rows = pltpu.make_async_copy(
        values.at[:, pl.ds(pl.multiple_of(head * FEATS, LANES), FEATS)],
        rows.at[head],
        local_sem.at[7],
    )
    own_rows.start()
    own_weight = pltpu.make_async_copy(
        weight, all_weight.at[z, x, :, :, own_lanes], local_sem.at[8]
    )
    own_weight.start()

    barrier = pltpu.get_barrier_semaphore()
    for step in range(1, 8):
        pl.semaphore_signal(
            barrier,
            inc=1,
            device_id=(ctx, lax.rem(head + step, 8)),
            device_id_type=MESH,
        )
    for step in range(1, 16):
        pl.semaphore_signal(
            barrier,
            inc=1,
            device_id=(lax.rem(ctx + step, 16), head),
            device_id_type=MESH,
        )
    pl.semaphore_wait(barrier, 22)

    def near_x(step):
        return z * 4 + lax.rem(x + step, 4)

    def near_z(step):
        return lax.rem(z + step, 4) * 4 + x

    offsets = [(0, 1), (1, 0), (1, 1), (3, 0), (3, 1), (2, 0), (2, 1)]
    order = [5, 6, 1, 2, 3, 4, 0]

    def head_at(step_y, step_core):
        return lax.rem(y + step_y, 4) * 2 + lax.rem(core + step_core, 2)

    value_copies = {}
    for number in order:
        step_y, step_core = offsets[number]
        target = head_at(step_y, step_core)
        value_copies[number] = copy(
            values.at[:, pl.ds(pl.multiple_of(target * FEATS, LANES), FEATS)],
            rows.at[head],
            a_send.at[number],
            a_recv.at[number],
            (ctx, target),
        )
        value_copies[number].start()

    first_copies = []
    for number, step in enumerate((2, 1, 3)):
        first_copies.append(
            copy(
                weight.at[0],
                all_weight.at[z, x, 0, :, own_lanes],
                w1_send.at[number],
                w1_recv.at[number],
                (near_x(step), head),
            )
        )
        first_copies.append(
            copy(
                weight.at[1],
                all_weight.at[z, x, 1, :, own_lanes],
                w1_send.at[3 + number],
                w1_recv.at[3 + number],
                (near_z(step), head),
            )
        )
    for item in first_copies:
        item.start()

    for load in loads:
        load.wait()
    spread = (
        (iota((HEADS_DEV, LANES), 1) % HEADS_DEV == iota((HEADS_DEV, LANES), 0))
        & (iota((HEADS_DEV, LANES), 1) < 100)
    ).astype(F32)
    lane_level = iota((CHUNK, LANES), 1) // HEADS_DEV
    causal = (iota((CHUNK, CHUNK), 0) >= iota((CHUNK, CHUNK), 1)) & (
        iota((CHUNK, CHUNK), 0) // 64 == iota((CHUNK, CHUNK), 1) // 64
    )
    causal_f32 = causal.astype(F32)
    first_half = iota((CHUNK, CHUNK), 1) < 64

    @pl.loop(0, CHUNKS)
    def _(j):
        tokens = pl.ds(pl.multiple_of(j * CHUNK, CHUNK), CHUNK)
        part = exact(causal_f32, exact(decay[tokens, :], spread))
        within[j] = part
        stretch[pl.ds(j * 2, 1), :] = part[63:64, :]
        stretch[pl.ds(j * 2 + 1, 1), :] = part[127:128, :]

    sums = stretch[...]
    total_row = jnp.sum(sums, axis=0, keepdims=True)
    totals[ctx] = jnp.broadcast_to(total_row, (8, LANES))
    total_copies = []
    for step in range(1, 16):
        total_copies.append(
            copy(
                totals.at[ctx],
                totals.at[ctx],
                t_send.at[step],
                t_recv.at[step],
                (lax.rem(ctx + step, 16), head),
            )
        )
        total_copies[-1].start()

    for level in range(10):
        source = iota((256, FEATS), 0) % LANES
        target = iota((256, FEATS), 1) // WIDTH + level * HEADS_DEV
        expander[level] = (source == target).astype(F32).astype(BF16)

    late = iota((16, 16), 0)
    early = iota((16, 16), 1)
    small_level = iota((16, LANES), 1) // HEADS_DEV
    prefix = jnp.zeros((16, LANES), F32)
    for size, low, high in ((2, 2, 3), (4, 3, 4), (8, 4, 5), (16, 5, 9)):
        before = ((late // size == early // size) & (early < late)).astype(F32)
        prefix = jnp.where(
            (small_level >= low) & (small_level < high), exact(before, sums), prefix
        )
    stretch[...] = prefix

    block = iota((32, 16), 0)
    piece = iota((32, 16), 1)
    pick = (block < 16) & (piece == block)
    pick = pick | (
        (block >= 16) & (block < 20) & (piece // 2 == (block - 16) * 2 + 1)
    )
    pick = pick | (
        (block >= 20) & (block < 22) & (piece // 4 == (block - 20) * 2 + 1)
    )
    pick = pick | ((block == 22) & (piece >= 8))
    row_factors[...] = dot(
        split(jnp.exp(exact(pick.astype(F32), sums))), expander[0]
    )

    table_rows = exact(
        table[:, 0, :], jnp.where(iota((HEADS_DEV, LANES), 1) // HEADS_DEV == 0, spread, 0.0)
    )
    for level in range(1, 9):
        table_rows = table_rows + exact(
            table[:, level, :],
            jnp.where(iota((HEADS_DEV, LANES), 1) // HEADS_DEV == level, spread, 0.0),
        )
    class_rows = iota((32, CHUNK), 0)
    lift_lane = (lane_level == LIFT).astype(F32)
    second_row = iota((CHUNK, LANES), 0) // 64

    @pl.loop(0, CHUNKS)
    def _(j):
        onehot = (class_rows == classes[pl.ds(j, 1), :]).astype(F32)
        weights = exact(onehot, table_rows, TN) + lift_lane
        part = within[j]
        start = jnp.where(
            second_row == 0, stretch[pl.ds(j * 2, 1), :], stretch[pl.ds(j * 2 + 1, 1), :]
        )
        exponent = jnp.where(lane_level == LIFT, -part, part + start)
        bit = jnp.where(
            lane_level == 1,
            second_row,
            jnp.where(
                lane_level == 2,
                lax.rem(j, 2),
                jnp.where(
                    lane_level == 3,
                    lax.rem(j // 2, 2),
                    jnp.where(lane_level == 4, j // 4, 1),
                ),
            ),
        )
        factors[j] = split(jnp.where(bit == 1, jnp.exp(exponent) * weights, 0.0))

    skip_row = dot(split(exact(skip[...], spread)), expander[0])

    own_weight.wait()
    for item in first_copies:
        item.wait_recv()
    second_copies = []
    forward_copies = []
    for number, step in enumerate((2, 1, 3)):
        second_copies.append(
            copy(
                all_weight.at[z, :, 0, :, own_lanes],
                all_weight.at[z, :, 0, :, own_lanes],
                w2_send.at[number],
                w2_recv.at[number],
                (near_z(step), head),
            )
        )
        second_copies.append(
            copy(
                all_weight.at[:, x, 1, :, own_lanes],
                all_weight.at[:, x, 1, :, own_lanes],
                w2_send.at[3 + number],
                w2_recv.at[3 + number],
                (near_x(step), head),
            )
        )
    for item in second_copies:
        item.start()

    def forward(slab, number):
        item = copy(
            slab(own_lanes),
            slab(own_lanes),
            wf_send.at[number],
            wf_recv.at[number],
            (ctx, partner),
        )
        item.start()
        forward_copies.append(item)

    forward(lambda lanes: all_weight.at[z, :, 0, :, lanes], 0)
    forward(lambda lanes: all_weight.at[:, x, 1, :, lanes], 1)

    def chunk_work(j):
        inputs = rows[j].astype(F32)
        factor = factors[j]
        tokens = pl.ds(pl.multiple_of(j * CHUNK, CHUNK), CHUNK)
        incoming = entering[tokens, :]
        reader = leaving[tokens, :]
        lifted = (dot(factor, expander[LIFT]) * inputs).astype(BF16)
        scores = jnp.where(causal, dot(reader, incoming, NT), 0.0)
        score_high = scores.astype(BF16)
        score_low = (scores - score_high.astype(F32)).astype(BF16)
        turned = incoming.astype(F32).T
        lower = jnp.where(first_half, turned, 0.0).astype(BF16)
        upper = jnp.where(first_half, 0.0, turned).astype(BF16)
        direct = dot(score_high, lifted) + dot(score_low, lifted)
        lower_state = row_factors[pl.ds(j * 2, 1), :] * dot(lower, lifted)
        pair_state[j] = row_factors[pl.ds(j * 2 + 1, 1), :] * (
            lower_state + dot(upper, lifted)
        )
        gained = dot(reader, lower_state.astype(BF16))
        output[j] = (
            dot(factor, expander[0]) * direct
            + dot(factor, expander[1]) * gained
            + skip_row * inputs
        )

    own_rows.wait()
    chunk_work(head)
    for number in range(7):
        step_y, step_core = offsets[number]
        origin = lax.rem(y + 4 - step_y, 4) * 2 + lax.rem(core + 2 - step_core, 2)
        copy(
            rows.at[origin],
            rows.at[origin],
            a_send.at[number],
            a_recv.at[number],
            (ctx, origin),
        ).wait_recv()

    @pl.loop(1, CHUNKS)
    def _(step):
        chunk_work(lax.rem(head + step, CHUNKS))

    for group in range(4):
        quad_state[group] = (
            row_factors[16 + group : 17 + group, :] * pair_state[2 * group]
            + pair_state[2 * group + 1]
        )
    for group in range(2):
        half_state[group] = (
            row_factors[20 + group : 21 + group, :] * quad_state[2 * group]
            + quad_state[2 * group + 1]
        )
    ring_x[x] = (row_factors[22:23, :] * half_state[0] + half_state[1]).astype(BF16)
    x_copies = []
    for number, step in enumerate((2, 1, 3)):
        x_copies.append(
            copy(
                ring_x.at[x],
                ring_x.at[x],
                x_send.at[number],
                x_recv.at[number],
                (near_x(step), head),
            )
        )
        x_copies[-1].start()

    @pl.loop(0, 4)
    def _(group):
        for level in (2, 3, 4):
            if level == 2:
                j = group * 2 + 1
                state = pair_state[group * 2]
            elif level == 3:
                j = 2 + lax.rem(group, 2) + 4 * (group // 2)
                state = quad_state[(group // 2) * 2]
            else:
                j = 4 + group
                state = half_state[0]
            tokens = pl.ds(pl.multiple_of(j * CHUNK, CHUNK), CHUNK)
            output[j] = output[j] + dot(factors[j], expander[level]) * dot(
                leaving[tokens, :], state.astype(BF16)
            )

    for step in range(1, 16):
        origin = lax.rem(ctx + 16 - step, 16)
        copy(
            totals.at[origin], totals.at[origin], t_send.at[step], t_recv.at[step], (origin, head)
        ).wait_recv()
    every_total = jnp.concatenate([totals[d][0:1, :] for d in range(16)], axis=0)
    row = iota((32, 16), 0)
    shard = iota((32, 16), 1)
    kind = row // 4
    slot = row % 4
    shard_x = shard % 4
    shard_z = shard // 4
    same_z = shard_z == z
    counted = ((kind == 1) & same_z & (shard_x > slot) & (shard_x < x)) | (
        (kind == 2) & same_z & (shard_x > slot)
    )
    counted = counted | ((kind >= 3) & (kind < 5) & same_z & (shard_x < x))
    counted = counted | ((kind == 4) & (shard_z > slot) & (shard_z < z))
    row = iota((32, LANES), 0)
    kind = row // 4
    slot = row % 4
    used = ((kind == 0) & (slot == x - 1) & (lax.rem(x, 2) == 1)) | (
        (kind == 1) & (x >= 2) & (slot < 2)
    )
    used = used | (kind == 2)
    used = used | ((kind == 3) & (slot == z - 1) & (lax.rem(z, 2) == 1))
    used = used | ((kind == 4) & (z >= 2) & (slot < 2))
    mix = jnp.where(used, jnp.exp(exact(counted.astype(F32), every_total)), 0.0)
    mix_factors[...] = dot(split(mix), expander[0])

    for number, step in enumerate((2, 1, 3)):
        origin = lax.rem(x + 4 - step, 4)
        copy(
            ring_x.at[origin],
            ring_x.at[origin],
            x_send.at[number],
            x_recv.at[number],
            (z * 4 + origin, head),
        ).wait_recv()
    first = jnp.zeros((STATE, FEATS), F32)
    second = jnp.zeros((STATE, FEATS), F32)
    merged = jnp.zeros((STATE, FEATS), F32)
    for source in range(4):
        state = ring_x[source].astype(F32)
        first = first + mix_factors[source : source + 1, :] * state
        second = second + mix_factors[4 + source : 5 + source, :] * state
        merged = merged + mix_factors[8 + source : 9 + source, :] * state
    ring_z[z] = merged.astype(BF16)
    z_copies = []
    for number, step in enumerate((2, 1, 3)):
        z_copies.append(
            copy(
                ring_z.at[z],
                ring_z.at[z],
                z_send.at[number],
                z_recv.at[number],
                (near_z(step), head),
            )
        )
        z_copies[-1].start()
    buckets[0] = first.astype(BF16)
    buckets[1] = second.astype(BF16)

    def read_levels(j, low):
        tokens = pl.ds(pl.multiple_of(j * CHUNK, CHUNK), CHUNK)
        reader = leaving[tokens, :]
        factor = factors[j]
        return dot(factor, expander[low]) * dot(reader, buckets[0]) + dot(
            factor, expander[low + 1]
        ) * dot(reader, buckets[1])

    @pl.loop(0, CHUNKS)
    def _(j):
        output[j] = output[j] + read_levels(j, 5)

    for number, step in enumerate((2, 1, 3)):
        from_z = lax.rem(z + 4 - step, 4)
        copy(
            all_weight.at[from_z, :, 0, :, own_lanes],
            all_weight.at[from_z, :, 0, :, own_lanes],
            w2_send.at[number],
            w2_recv.at[number],
            (from_z * 4 + x, head),
        ).wait_recv()
        forward(lambda lanes: all_weight.at[from_z, :, 0, :, lanes], 2 + number)
        from_x = lax.rem(x + 4 - step, 4)
        copy(
            all_weight.at[:, from_x, 1, :, own_lanes],
            all_weight.at[:, from_x, 1, :, own_lanes],
            w2_send.at[3 + number],
            w2_recv.at[3 + number],
            (z * 4 + from_x, head),
        ).wait_recv()
        forward(lambda lanes: all_weight.at[:, from_x, 1, :, lanes], 5 + number)

    for number, step in enumerate((2, 1, 3)):
        origin = lax.rem(z + 4 - step, 4)
        copy(
            ring_z.at[origin],
            ring_z.at[origin],
            z_send.at[number],
            z_recv.at[number],
            (origin * 4 + x, head),
        ).wait_recv()
    first = jnp.zeros((STATE, FEATS), F32)
    second = jnp.zeros((STATE, FEATS), F32)
    for source in range(4):
        state = ring_z[source].astype(F32)
        first = first + mix_factors[12 + source : 13 + source, :] * state
        second = second + mix_factors[16 + source : 17 + source, :] * state
    buckets[0] = first.astype(BF16)
    buckets[1] = second.astype(BF16)

    same_head = (
        iota((256, LANES), 0) % LANES // WIDTH == iota((256, LANES), 1) // WIDTH
    ).astype(F32).astype(BF16)

    def finish(j):
        total = output[j] + read_levels(j, 7)
        pieces = []
        for group in range(FEATS // LANES):
            part = total[:, group * LANES : (group + 1) * LANES]
            mean_square = dot(split(part * part), same_head) * (1.0 / WIDTH)
            scaled = part * lax.rsqrt(mean_square + EPSILON)
            pieces.append(scaled * gain[:, group * LANES : (group + 1) * LANES])
        return jnp.concatenate(pieces, axis=1).astype(BF16)

    @pl.loop(0, 4)
    def _(step):
        target = lax.rem(y + step, 4)
        normed_send[step] = finish(target * 2 + (1 - core))

    normed_copies = []
    for step in range(4):
        normed_copies.append(
            copy(
                normed_send.at[step],
                normed_all.at[step, :, own_lanes],
                n_send.at[step],
                n_recv.at[step],
                (ctx, partner),
            )
        )
        normed_copies[-1].start()

    @pl.loop(0, 4)
    def _(step):
        target = lax.rem(y + step, 4)
        normed_all[step, :, own_lanes] = finish(target * 2 + core)

    for item in normed_copies:
        item.wait_recv()

    slabs = [
        lambda lanes: all_weight.at[z, :, 0, :, lanes],
        lambda lanes: all_weight.at[:, x, 1, :, lanes],
    ]
    for number, step in enumerate((2, 1, 3)):
        from_z = lax.rem(z + 4 - step, 4)
        slabs.append(lambda lanes, at=from_z: all_weight.at[at, :, 0, :, lanes])
    for number, step in enumerate((2, 1, 3)):
        from_x = lax.rem(x + 4 - step, 4)
        slabs.append(lambda lanes, at=from_x: all_weight.at[:, at, 1, :, lanes])
    for number, slab in enumerate(slabs):
        copy(
            slab(other_lanes),
            slab(other_lanes),
            wf_send.at[number],
            wf_recv.at[number],
            (ctx, partner),
        ).wait_recv()

    tile = OUTS // 4
    partial_copies = []
    for quarter in range(4):
        block_weight = all_weight[quarter].reshape(tile, 2 * FEATS)
        product = dot(normed_all[...].reshape(4 * CHUNK, 2 * FEATS), block_weight, NT)
        own_sum[:, quarter * tile : (quarter + 1) * tile] = product[:CHUNK]
        for number, step in enumerate((2, 1, 3)):
            partial_send[number, quarter] = product[
                step * CHUNK : (step + 1) * CHUNK
            ].astype(BF16)
            item = copy(
                partial_send.at[number, quarter],
                partial_recv.at[number, quarter],
                p_send.at[number, quarter],
                p_recv.at[number, quarter],
                (ctx, lax.rem(y + step, 4) * 2 + core),
            )
            item.start()
            partial_copies.append(item)
    for quarter in range(4):
        for number in range(3):
            partial_copies[quarter * 3 + number].wait_recv()
        columns = slice(quarter * tile, (quarter + 1) * tile)
        result[:, columns] = (
            own_sum[:, columns]
            + partial_recv[0, quarter].astype(F32)
            + partial_recv[1, quarter].astype(F32)
            + partial_recv[2, quarter].astype(F32)
        ).astype(BF16)

    for number in order:
        value_copies[number].wait_send()
    for item in (
        first_copies
        + total_copies
        + second_copies
        + forward_copies
        + x_copies
        + z_copies
        + normed_copies
        + partial_copies
    ):
        item.wait_send()


def on_device(
    values,
    state_in,
    state_out,
    log_decay,
    level_class,
    level_table,
    skip_gain,
    norm_gain,
    out_weight,
):
    columns = out_weight.shape[1]
    weight = out_weight.T.reshape(2, columns // 2, FEATS)
    anywhere = pl.BlockSpec(memory_space=pl.ANY)
    dma = pltpu.SemaphoreType.DMA
    return pl.pallas_call(
        kernel,
        out_shape=jax.ShapeDtypeStruct((CHUNK, OUTS), BF16),
        in_specs=[anywhere] * 9,
        out_specs=pl.BlockSpec(memory_space=pltpu.VMEM),
        scratch_shapes=[
            pltpu.VMEM((CHUNKS, CHUNK, FEATS), BF16),
            pltpu.VMEM((CHUNKS * CHUNK, STATE), BF16),
            pltpu.VMEM((CHUNKS * CHUNK, STATE), BF16),
            pltpu.VMEM((CHUNKS * CHUNK, HEADS_DEV), F32),
            pltpu.VMEM((CHUNKS, CHUNK), jnp.int32),
            pltpu.VMEM((32, 9, HEADS_DEV), F32),
            pltpu.VMEM((1, HEADS_DEV), F32),
            pltpu.VMEM((1, FEATS), F32),
            pltpu.VMEM((4, 4, 2, 80, 2 * FEATS), BF16),
            pltpu.VMEM((10, 256, FEATS), BF16),
            pltpu.VMEM((CHUNKS, CHUNK, LANES), F32),
            pltpu.VMEM((16, LANES), F32),
            pltpu.VMEM((CHUNKS, CHUNK, 2 * LANES), BF16),
            pltpu.VMEM((16, 8, LANES), F32),
            pltpu.VMEM((32, FEATS), F32),
            pltpu.VMEM((32, FEATS), F32),
            pltpu.VMEM((CHUNKS, STATE, FEATS), F32),
            pltpu.VMEM((4, STATE, FEATS), F32),
            pltpu.VMEM((2, STATE, FEATS), F32),
            pltpu.VMEM((CHUNKS, CHUNK, FEATS), F32),
            pltpu.VMEM((4, STATE, FEATS), BF16),
            pltpu.VMEM((4, STATE, FEATS), BF16),
            pltpu.VMEM((2, STATE, FEATS), BF16),
            pltpu.VMEM((4, CHUNK, FEATS), BF16),
            pltpu.VMEM((4, CHUNK, 2 * FEATS), BF16),
            pltpu.VMEM((CHUNK, OUTS), F32),
            pltpu.VMEM((3, 4, CHUNK, OUTS // 4), BF16),
            pltpu.VMEM((3, 4, CHUNK, OUTS // 4), BF16),
            dma((9,)),
            dma((7,)),
            dma((7,)),
            dma((6,)),
            dma((6,)),
            dma((6,)),
            dma((6,)),
            dma((8,)),
            dma((8,)),
            dma((16,)),
            dma((16,)),
            dma((3,)),
            dma((3,)),
            dma((3,)),
            dma((3,)),
            dma((4,)),
            dma((4,)),
            dma((3, 4)),
            dma((3, 4)),
        ],
        compiler_params=pltpu.CompilerParams(
            collective_id=0,
            has_side_effects=True,
            vmem_limit_bytes=60 * 1024 * 1024,
        ),
        name="layer",
    )(
        values,
        state_in,
        state_out,
        log_decay,
        level_class.reshape(CHUNKS, CHUNK),
        level_table,
        skip_gain.reshape(1, -1),
        norm_gain.reshape(1, -1),
        weight,
    )


def solution(mesh):
    return jax.shard_map(
        on_device,
        mesh=mesh,
        in_specs=(
            P(("ctx", "head"), None),
            P("ctx", None),
            P("ctx", None),
            P("ctx", "head"),
            P("ctx"),
            P(None, None, "head"),
            P("head"),
            P("head"),
            P("head", "ctx"),
        ),
        out_specs=P(("ctx", "head"), None),
        check_vma=False,
    )
```

profile of v0, /device:TPU:1, one launch (start us, length us, event | category | flops | bytes accessed | tf_op | source)
XLA Modules:
  0.0 97.4 jit_solution(12763362414853279603)
XLA Ops:
  0.0 1.3 %reshape.14.norm_gain = f32[1,640]{1,0:T(1,128)} reshape(f32[640]{0:T(1024)} %param.16) | data formatting | bytes 5120 | tf_op jit(solution)/shard_map/reshape | solution.py:746
  1.3 1.7 %copy.11.level_table = f32[32,9,10]{2,1,0:T(8,128)} copy(f32[32,9,10]{0,2,1:T(8,128)} %param.14) | data formatting | bytes 23040 | tf_op args[5]
  3.0 1.9 %copy.10.log_decay = f32[1024,10]{1,0:T(8,128)} copy(f32[1024,10]{0,1:T(8,128)} %param.12) | data formatting | bytes 81920 | tf_op args[3]
  4.9 90.6 %layer.1 = bf16[128,2560]{1,0:T(8,128)(2,1)} custom-call(bf16[128,5120]{1,0:T(8,128)(2,1)} %values.1, bf16[1024,128]{1,0:T(8,128)(2,1)} %state_in.1, bf16[1024,128]{1,0:T(8,128)(2,1)} %state_out.1, f32[1024,10]{1,0:T(8,128)} %copy.10.log_decay, s32[8,128]{1,0:T(8,128)} %bitcast.6, f32[32,9,10]{2,1,0:T(8,128)} %copy.11.level_table, f32[1,10]{1,0:T(1,128)} %bitcast.7, ...), custom_call_target="tpu_custom_call" | custom-call | tf_op jit(solution)/shard_map/layer/pallas_call | solution.py:678
  95.5 2.0 %copy.13 = bf16[128,2560]{1,0:T(8,128)(2,1)} copy(bf16[128,2560]{1,0:T(8,128)(2,1)} %layer.1) | data formatting | bytes 1310720
where the time goes:
time: 97.7 us; the launch traced here: 97.4 us
  Pallas kernels  90.6 us (93%)
  local copies, waits for them, and re-layouts  6.84 us (7%)
    pallas_call x1, Pallas kernels, on_device(): pl.pallas_call(kernel, out_shape=jax.ShapeDtypeStruct((CHUNK, OUTS), BF16...  90.6 us
    unnamed x3, local copies, waits for them, and re-layouts  5.56 us

commit v1 on v0

--- a/solution.py
+++ b/solution.py
@@ -19,6 +19,8 @@
 CHUNKS = 8
 OUTS = 2560
 LIFT = 9
+GROUPS = ((0, 384), (384, 640))
+TILE = OUTS // 4
 
 NT = (((1,), (1,)), ((), ()))
 TN = (((0,), (0,)), ((), ()))
@@ -37,10 +39,10 @@
     return lax.dot_general(a, b, dims, precision=PRECISE, preferred_element_type=F32)
 
 
-def split(value):
+def split(value, axis=1):
     high = value.astype(BF16)
     low = (value - high.astype(F32)).astype(BF16)
-    return jnp.concatenate([high, low], axis=1)
+    return jnp.concatenate([high, low], axis=axis)
 
 
 def kernel(
@@ -67,6 +69,8 @@
     within,
     stretch,
     factors,
+    mixers,
+    readers,
     totals,
     row_factors,
     mix_factors,
@@ -80,7 +84,9 @@
     normed_send,
     normed_all,
     own_sum,
+    held,
     partial_send,
+    relay_recv,
     partial_recv,
     local_sem,
     a_send,
@@ -99,6 +105,8 @@
     z_recv,
     n_send,
     n_recv,
+    r_send,
+    r_recv,
     p_send,
     p_recv,
 ):
@@ -138,14 +146,14 @@
         load.start()
     own_lanes = pl.ds(pl.multiple_of(core * FEATS, LANES), FEATS)
     other_lanes = pl.ds(pl.multiple_of((1 - core) * FEATS, LANES), FEATS)
-    own_rows = pltpu.make_async_copy(
-        values.at[:, pl.ds(pl.multiple_of(head * FEATS, LANES), FEATS)],
-        rows.at[head],
-        local_sem.at[7],
-    )
-    own_rows.start()
+    for number, (low, high) in enumerate(GROUPS):
+        pltpu.make_async_copy(
+            values.at[:, pl.ds(pl.multiple_of(head * FEATS + low, LANES), high - low)],
+            rows.at[head, :, low:high],
+            a_recv.at[number, 0],
+        ).start()
     own_weight = pltpu.make_async_copy(
-        weight, all_weight.at[z, x, :, :, own_lanes], local_sem.at[8]
+        weight, all_weight.at[z, x, :, :, own_lanes], local_sem.at[7]
     )
     own_weight.start()
 
@@ -172,24 +180,27 @@
     def near_z(step):
         return lax.rem(z + step, 4) * 4 + x
 
-    offsets = [(0, 1), (1, 0), (1, 1), (3, 0), (3, 1), (2, 0), (2, 1)]
-    order = [5, 6, 1, 2, 3, 4, 0]
-
-    def head_at(step_y, step_core):
-        return lax.rem(y + step_y, 4) * 2 + lax.rem(core + step_core, 2)
-
-    value_copies = {}
-    for number in order:
-        step_y, step_core = offsets[number]
-        target = head_at(step_y, step_core)
-        value_copies[number] = copy(
-            values.at[:, pl.ds(pl.multiple_of(target * FEATS, LANES), FEATS)],
-            rows.at[head],
-            a_send.at[number],
-            a_recv.at[number],
-            (ctx, target),
-        )
-        value_copies[number].start()
+    def step_of(number):
+        pair = number // 2
+        return pair + (pair // 2) * (1 - 2 * lax.rem(pair, 2)), lax.rem(number, 2)
+
+    value_copies = []
+    for group, (low, high) in enumerate(GROUPS):
+        for number in (6, 7, 2, 3, 4, 5, 1):
+            step_y, step_core = step_of(number)
+            target = lax.rem(y + step_y, 4) * 2 + lax.rem(core + step_core, 2)
+            value_copies.append(
+                copy(
+                    values.at[
+                        :, pl.ds(pl.multiple_of(target * FEATS + low, LANES), high - low)
+                    ],
+                    rows.at[head, :, low:high],
+                    a_send.at[group, number],
+                    a_recv.at[group, number],
+                    (ctx, target),
+                )
+            )
+            value_copies[-1].start()
 
     first_copies = []
     for number, step in enumerate((2, 1, 3)):
@@ -230,7 +241,7 @@
     @pl.loop(0, CHUNKS)
     def _(j):
         tokens = pl.ds(pl.multiple_of(j * CHUNK, CHUNK), CHUNK)
-        part = exact(causal_f32, exact(decay[tokens, :], spread))
+        part = exact(causal_f32, exact(decay[:, tokens], spread, TN))
         within[j] = part
         stretch[pl.ds(j * 2, 1), :] = part[63:64, :]
         stretch[pl.ds(j * 2 + 1, 1), :] = part[127:128, :]
@@ -281,13 +292,12 @@
         split(jnp.exp(exact(pick.astype(F32), sums))), expander[0]
     )
 
-    table_rows = exact(
-        table[:, 0, :], jnp.where(iota((HEADS_DEV, LANES), 1) // HEADS_DEV == 0, spread, 0.0)
-    )
-    for level in range(1, 9):
+    table_rows = jnp.zeros((32, LANES), F32)
+    for level in range(9):
         table_rows = table_rows + exact(
-            table[:, level, :],
+            table[level],
             jnp.where(iota((HEADS_DEV, LANES), 1) // HEADS_DEV == level, spread, 0.0),
+            TN,
         )
     class_rows = iota((32, CHUNK), 0)
     lift_lane = (lane_level == LIFT).astype(F32)
@@ -316,6 +326,18 @@
             ),
         )
         factors[j] = split(jnp.where(bit == 1, jnp.exp(exponent) * weights, 0.0))
+        tokens = pl.ds(pl.multiple_of(j * CHUNK, CHUNK), CHUNK)
+        incoming = entering[tokens, :]
+        reader = leaving[tokens, :]
+        readers[j] = jnp.concatenate([reader, reader], axis=1)
+        scores = jnp.where(causal, dot(reader, incoming, NT), 0.0)
+        score_high = scores.astype(BF16)
+        score_low = (scores - score_high.astype(F32)).astype(BF16)
+        turned = incoming.astype(F32).T
+        lower = jnp.where(first_half, turned, 0.0).astype(BF16)
+        upper = jnp.where(first_half, 0.0, turned).astype(BF16)
+        half = jnp.concatenate([score_high, score_low, lower, upper], axis=0)
+        mixers[j] = jnp.concatenate([half, half], axis=1)
 
     skip_row = dot(split(exact(skip[...], spread)), expander[0])
 
@@ -360,74 +382,116 @@
     forward(lambda lanes: all_weight.at[z, :, 0, :, lanes], 0)
     forward(lambda lanes: all_weight.at[:, x, 1, :, lanes], 1)
 
-    def chunk_work(j):
-        inputs = rows[j].astype(F32)
+    def chunk_work(j, low, high):
+        inputs = rows[j, :, low:high].astype(F32)
         factor = factors[j]
-        tokens = pl.ds(pl.multiple_of(j * CHUNK, CHUNK), CHUNK)
-        incoming = entering[tokens, :]
-        reader = leaving[tokens, :]
-        lifted = (dot(factor, expander[LIFT]) * inputs).astype(BF16)
-        scores = jnp.where(causal, dot(reader, incoming, NT), 0.0)
-        score_high = scores.astype(BF16)
-        score_low = (scores - score_high.astype(F32)).astype(BF16)
-        turned = incoming.astype(F32).T
-        lower = jnp.where(first_half, turned, 0.0).astype(BF16)
-        upper = jnp.where(first_half, 0.0, turned).astype(BF16)
-        direct = dot(score_high, lifted) + dot(score_low, lifted)
-        lower_state = row_factors[pl.ds(j * 2, 1), :] * dot(lower, lifted)
-        pair_state[j] = row_factors[pl.ds(j * 2 + 1, 1), :] * (
-            lower_state + dot(upper, lifted)
-        )
-        gained = dot(reader, lower_state.astype(BF16))
-        output[j] = (
-            dot(factor, expander[0]) * direct
-            + dot(factor, expander[1]) * gained
-            + skip_row * inputs
-        )
-
-    own_rows.wait()
-    chunk_work(head)
-    for number in range(7):
-        step_y, step_core = offsets[number]
-        origin = lax.rem(y + 4 - step_y, 4) * 2 + lax.rem(core + 2 - step_core, 2)
-        copy(
-            rows.at[origin],
-            rows.at[origin],
-            a_send.at[number],
-            a_recv.at[number],
-            (ctx, origin),
-        ).wait_recv()
-
-    @pl.loop(1, CHUNKS)
-    def _(step):
-        chunk_work(lax.rem(head + step, CHUNKS))
-
-    for group in range(4):
-        quad_state[group] = (
-            row_factors[16 + group : 17 + group, :] * pair_state[2 * group]
-            + pair_state[2 * group + 1]
-        )
-    for group in range(2):
-        half_state[group] = (
-            row_factors[20 + group : 21 + group, :] * quad_state[2 * group]
-            + quad_state[2 * group + 1]
-        )
-    ring_x[x] = (row_factors[22:23, :] * half_state[0] + half_state[1]).astype(BF16)
+        lifted = split(dot(factor, expander[LIFT, :, low:high]) * inputs, 0)
+        product = dot(mixers[j], lifted)
+        lower_state = row_factors[pl.ds(j * 2, 1), low:high] * product[256:384]
+        pair_state[j, :, low:high] = row_factors[pl.ds(j * 2 + 1, 1), low:high] * (
+            lower_state + product[384:512]
+        )
+        gained = dot(readers[j], split(lower_state, 0))
+        output[j, :, low:high] = (
+            dot(factor, expander[0, :, low:high]) * (product[:128] + product[128:256])
+            + dot(factor, expander[1, :, low:high]) * gained
+            + skip_row[:, low:high] * inputs
+        )
+
     x_copies = []
-    for number, step in enumerate((2, 1, 3)):
-        x_copies.append(
+    for group, (low, high) in enumerate(GROUPS):
+
+        @pl.loop(0, CHUNKS)
+        def _(number):
+            step_y, step_core = step_of(number)
+            origin = lax.rem(y + 4 - step_y, 4) * 2 + lax.rem(core + 2 - step_core, 2)
+            pltpu.make_async_copy(
+                rows.at[origin, :, low:high],
+                rows.at[origin, :, low:high],
+                a_recv.at[group, number],
+            ).wait()
+            chunk_work(origin, low, high)
+
+        for quad in range(4):
+            quad_state[quad, :, low:high] = (
+                row_factors[16 + quad : 17 + quad, low:high]
+                * pair_state[2 * quad, :, low:high]
+                + pair_state[2 * quad + 1, :, low:high]
+            )
+        for half in range(2):
+            half_state[half, :, low:high] = (
+                row_factors[20 + half : 21 + half, low:high]
+                * quad_state[2 * half, :, low:high]
+                + quad_state[2 * half + 1, :, low:high]
+            )
+        ring_x[x, :, low:high] = (
+            row_factors[22:23, low:high] * half_state[0, :, low:high]
+            + half_state[1, :, low:high]
+        ).astype(BF16)
+        for number, step in enumerate((2, 1, 3)):
+            x_copies.append(
+                copy(
+                    ring_x.at[x, :, low:high],
+                    ring_x.at[x, :, low:high],
+                    x_send.at[group, number],
+                    x_recv.at[group, number],
+                    (near_x(step), head),
+                )
+            )
+            x_copies[-1].start()
+        if group == 0:
+            for step in range(1, 16):
+                origin = lax.rem(ctx + 16 - step, 16)
+                copy(
+                    totals.at[origin],
+                    totals.at[origin],
+                    t_send.at[step],
+                    t_recv.at[step],
+                    (origin, head),
+                ).wait_recv()
+            every_total = jnp.concatenate([totals[d][0:1, :] for d in range(16)], axis=0)
+            row = iota((32, 16), 0)
+            shard = iota((32, 16), 1)
+            kind = row // 4
+            slot = row % 4
+            shard_x = shard % 4
+            shard_z = shard // 4
+            same_z = shard_z == z
+            counted = (kind == 1) & same_z & (shard_x > slot) & (shard_x < x)
+            counted = counted | ((kind == 2) & same_z & (shard_x > slot))
+            counted = counted | ((kind >= 3) & (kind < 5) & same_z & (shard_x < x))
+            counted = counted | ((kind == 4) & (shard_z > slot) & (shard_z < z))
+            row = iota((32, LANES), 0)
+            kind = row // 4
+            slot = row % 4
+            used = (kind == 0) & (slot == x - 1) & (lax.rem(x, 2) == 1)
+            used = used | ((kind == 1) & (x >= 2) & (slot < 2))
+            used = used | (kind == 2)
+            used = used | ((kind == 3) & (slot == z - 1) & (lax.rem(z, 2) == 1))
+            used = used | ((kind == 4) & (z >= 2) & (slot < 2))
+            mix = jnp.where(used, jnp.exp(exact(counted.astype(F32), every_total)), 0.0)
+            mix_factors[...] = dot(split(mix), expander[0])
+
+    def mixed(ring, start, low, high):
+        total = jnp.zeros((STATE, high - low), F32)
+        for source in range(4):
+            total = total + mix_factors[
+                start + source : start + source + 1, low:high
+            ] * ring[source, :, low:high].astype(F32)
+        return total
+
+    def hear(ring, recv, group, low, high, position, device):
+        for number, step in enumerate((2, 1, 3)):
+            origin = lax.rem(position + 4 - step, 4)
             copy(
-                ring_x.at[x],
-                ring_x.at[x],
-                x_send.at[number],
-                x_recv.at[number],
-                (near_x(step), head),
-            )
-        )
-        x_copies[-1].start()
-
-    @pl.loop(0, 4)
-    def _(group):
+                ring.at[origin, :, low:high],
+                ring.at[origin, :, low:high],
+                x_send.at[group, number],
+                recv.at[group, number],
+                (device(origin), head),
+            ).wait_recv()
+
+    def read_local(group):
         for level in (2, 3, 4):
             if level == 2:
                 j = group * 2 + 1
@@ -438,78 +502,33 @@
             else:
                 j = 4 + group
                 state = half_state[0]
-            tokens = pl.ds(pl.multiple_of(j * CHUNK, CHUNK), CHUNK)
             output[j] = output[j] + dot(factors[j], expander[level]) * dot(
-                leaving[tokens, :], state.astype(BF16)
-            )
-
-    for step in range(1, 16):
-        origin = lax.rem(ctx + 16 - step, 16)
-        copy(
-            totals.at[origin], totals.at[origin], t_send.at[step], t_recv.at[step], (origin, head)
-        ).wait_recv()
-    every_total = jnp.concatenate([totals[d][0:1, :] for d in range(16)], axis=0)
-    row = iota((32, 16), 0)
-    shard = iota((32, 16), 1)
-    kind = row // 4
-    slot = row % 4
-    shard_x = shard % 4
-    shard_z = shard // 4
-    same_z = shard_z == z
-    counted = ((kind == 1) & same_z & (shard_x > slot) & (shard_x < x)) | (
-        (kind == 2) & same_z & (shard_x > slot)
-    )
-    counted = counted | ((kind >= 3) & (kind < 5) & same_z & (shard_x < x))
-    counted = counted | ((kind == 4) & (shard_z > slot) & (shard_z < z))
-    row = iota((32, LANES), 0)
-    kind = row // 4
-    slot = row % 4
-    used = ((kind == 0) & (slot == x - 1) & (lax.rem(x, 2) == 1)) | (
-        (kind == 1) & (x >= 2) & (slot < 2)
-    )
-    used = used | (kind == 2)
-    used = used | ((kind == 3) & (slot == z - 1) & (lax.rem(z, 2) == 1))
-    used = used | ((kind == 4) & (z >= 2) & (slot < 2))
-    mix = jnp.where(used, jnp.exp(exact(counted.astype(F32), every_total)), 0.0)
-    mix_factors[...] = dot(split(mix), expander[0])
-
-    for number, step in enumerate((2, 1, 3)):
-        origin = lax.rem(x + 4 - step, 4)
-        copy(
-            ring_x.at[origin],
-            ring_x.at[origin],
-            x_send.at[number],
-            x_recv.at[number],
-            (z * 4 + origin, head),
-        ).wait_recv()
-    first = jnp.zeros((STATE, FEATS), F32)
-    second = jnp.zeros((STATE, FEATS), F32)
-    merged = jnp.zeros((STATE, FEATS), F32)
-    for source in range(4):
-        state = ring_x[source].astype(F32)
-        first = first + mix_factors[source : source + 1, :] * state
-        second = second + mix_factors[4 + source : 5 + source, :] * state
-        merged = merged + mix_factors[8 + source : 9 + source, :] * state
-    ring_z[z] = merged.astype(BF16)
+                readers[j], split(state, 0)
+            )
+
     z_copies = []
-    for number, step in enumerate((2, 1, 3)):
-        z_copies.append(
-            copy(
-                ring_z.at[z],
-                ring_z.at[z],
-                z_send.at[number],
-                z_recv.at[number],
-                (near_z(step), head),
-            )
-        )
-        z_copies[-1].start()
-    buckets[0] = first.astype(BF16)
-    buckets[1] = second.astype(BF16)
+    for group, (low, high) in enumerate(GROUPS):
+        hear(ring_x, x_recv, group, low, high, x, lambda origin: z * 4 + origin)
+        ring_z[z, :, low:high] = mixed(ring_x, 8, low, high).astype(BF16)
+        for number, step in enumerate((2, 1, 3)):
+            z_copies.append(
+                copy(
+                    ring_z.at[z, :, low:high],
+                    ring_z.at[z, :, low:high],
+                    z_send.at[group, number],
+                    z_recv.at[group, number],
+                    (near_z(step), head),
+                )
+            )
+            z_copies[-1].start()
+        buckets[0, :, low:high] = split(mixed(ring_x, 0, low, high), 0)
+        buckets[1, :, low:high] = split(mixed(ring_x, 4, low, high), 0)
+        if group == 0:
+            pl.loop(0, 4)(read_local)
 
     def read_levels(j, low):
-        tokens = pl.ds(pl.multiple_of(j * CHUNK, CHUNK), CHUNK)
-        reader = leaving[tokens, :]
         factor = factors[j]
+        reader = readers[j]
         return dot(factor, expander[low]) * dot(reader, buckets[0]) + dot(
             factor, expander[low + 1]
         ) * dot(reader, buckets[1])
@@ -538,23 +557,10 @@
         ).wait_recv()
         forward(lambda lanes: all_weight.at[:, from_x, 1, :, lanes], 5 + number)
 
-    for number, step in enumerate((2, 1, 3)):
-        origin = lax.rem(z + 4 - step, 4)
-        copy(
-            ring_z.at[origin],
-            ring_z.at[origin],
-            z_send.at[number],
-            z_recv.at[number],
-            (origin * 4 + x, head),
-        ).wait_recv()
-    first = jnp.zeros((STATE, FEATS), F32)
-    second = jnp.zeros((STATE, FEATS), F32)
-    for source in range(4):
-        state = ring_z[source].astype(F32)
-        first = first + mix_factors[12 + source : 13 + source, :] * state
-        second = second + mix_factors[16 + source : 17 + source, :] * state
-    buckets[0] = first.astype(BF16)
-    buckets[1] = second.astype(BF16)
+    for group, (low, high) in enumerate(GROUPS):
+        hear(ring_z, z_recv, group, low, high, z, lambda origin: origin * 4 + x)
+        buckets[0, :, low:high] = split(mixed(ring_z, 12, low, high), 0)
+        buckets[1, :, low:high] = split(mixed(ring_z, 16, low, high), 0)
 
     same_head = (
         iota((256, LANES), 0) % LANES // WIDTH == iota((256, LANES), 1) // WIDTH
@@ -570,32 +576,30 @@
             pieces.append(scaled * gain[:, group * LANES : (group + 1) * LANES])
         return jnp.concatenate(pieces, axis=1).astype(BF16)
 
-    @pl.loop(0, 4)
-    def _(step):
-        target = lax.rem(y + step, 4)
-        normed_send[step] = finish(target * 2 + (1 - core))
+    def place_chip(place):
+        return lax.rem(y + (2, 1, 3, 0)[place], 4)
 
     normed_copies = []
-    for step in range(4):
+
+    def hand_over(place):
+        normed_send[place] = finish(place_chip(place) * 2 + (1 - core))
         normed_copies.append(
             copy(
-                normed_send.at[step],
-                normed_all.at[step, :, own_lanes],
-                n_send.at[step],
-                n_recv.at[step],
+                normed_send.at[place],
+                normed_all.at[place, :, own_lanes],
+                n_send.at[place],
+                n_recv.at[place],
                 (ctx, partner),
             )
         )
         normed_copies[-1].start()
 
-    @pl.loop(0, 4)
-    def _(step):
-        target = lax.rem(y + step, 4)
-        normed_all[step, :, own_lanes] = finish(target * 2 + core)
-
-    for item in normed_copies:
-        item.wait_recv()
-
+    def keep(place):
+        normed_all[place, :, own_lanes] = finish(place_chip(place) * 2 + core)
+
+    hand_over(0)
+    keep(0)
+    hand_over(1)
     slabs = [
         lambda lanes: all_weight.at[z, :, 0, :, lanes],
         lambda lanes: all_weight.at[:, x, 1, :, lanes],
@@ -615,40 +619,93 @@
             (ctx, partner),
         ).wait_recv()
 
-    tile = OUTS // 4
+    up = (ctx, lax.rem(y + 1, 4) * 2 + core)
+    down = (ctx, lax.rem(y + 3, 4) * 2 + core)
     partial_copies = []
+
+    def product(first_place, last_place, quarter):
+        count = last_place - first_place
+        return dot(
+            normed_all[first_place:last_place].reshape(count * CHUNK, 2 * FEATS),
+            all_weight[quarter].reshape(TILE, 2 * FEATS),
+            NT,
+        )
+
+    def send(value, place, quarter, target, send_sems, recv_sems, device):
+        partial_send[place, quarter] = value.astype(BF16)
+        item = copy(
+            partial_send.at[place, quarter], target, send_sems, recv_sems, device
+        )
+        item.start()
+        partial_copies.append(item)
+
+    normed_copies[0].wait_recv()
+    for quarter in (0, 2, 1, 3):
+        send(
+            product(0, 1, quarter),
+            0,
+            quarter,
+            relay_recv.at[quarter],
+            r_send.at[quarter],
+            r_recv.at[quarter],
+            up if quarter < 2 else down,
+        )
+    keep(1)
+    hand_over(2)
+    keep(2)
+    normed_copies[1].wait_recv()
+    normed_copies[2].wait_recv()
+
+    def send_near(value, place, quarter):
+        send(
+            value,
+            place,
+            quarter,
+            partial_recv.at[place - 1, quarter],
+            p_send.at[place - 1, quarter],
+            p_recv.at[place - 1, quarter],
+            up if place == 1 else down,
+        )
+
+    for quarter in (2, 0, 3, 1):
+        both = product(1, 3, quarter)
+        if quarter < 2:
+            held[quarter] = both[:CHUNK]
+            send_near(both[CHUNK:], 2, quarter)
+        else:
+            send_near(both[:CHUNK], 1, quarter)
+            held[quarter] = both[CHUNK:]
+    hand_over(3)
+    keep(3)
+    for quarter in (0, 2, 1, 3):
+        partial_copies[(0, 2, 1, 3).index(quarter)].wait_recv()
+        send_near(
+            held[quarter] + relay_recv[quarter].astype(F32),
+            1 if quarter < 2 else 2,
+            quarter,
+        )
+    normed_copies[3].wait_recv()
     for quarter in range(4):
-        block_weight = all_weight[quarter].reshape(tile, 2 * FEATS)
-        product = dot(normed_all[...].reshape(4 * CHUNK, 2 * FEATS), block_weight, NT)
-        own_sum[:, quarter * tile : (quarter + 1) * tile] = product[:CHUNK]
-        for number, step in enumerate((2, 1, 3)):
-            partial_send[number, quarter] = product[
-                step * CHUNK : (step + 1) * CHUNK
-            ].astype(BF16)
-            item = copy(
-                partial_send.at[number, quarter],
-                partial_recv.at[number, quarter],
-                p_send.at[number, quarter],
-                p_recv.at[number, quarter],
-                (ctx, lax.rem(y + step, 4) * 2 + core),
-            )
-            item.start()
-            partial_copies.append(item)
+        own_sum[:, quarter * TILE : (quarter + 1) * TILE] = product(3, 4, quarter)
     for quarter in range(4):
-        for number in range(3):
-            partial_copies[quarter * 3 + number].wait_recv()
-        columns = slice(quarter * tile, (quarter + 1) * tile)
+        for place in range(2):
+            copy(
+                partial_recv.at[place, quarter],
+                partial_recv.at[place, quarter],
+                p_send.at[place, quarter],
+                p_recv.at[place, quarter],
+                up,
+            ).wait_recv()
+        columns = slice(quarter * TILE, (quarter + 1) * TILE)
         result[:, columns] = (
             own_sum[:, columns]
             + partial_recv[0, quarter].astype(F32)
             + partial_recv[1, quarter].astype(F32)
-            + partial_recv[2, quarter].astype(F32)
         ).astype(BF16)
 
-    for number in order:
-        value_copies[number].wait_send()
     for item in (
-        first_copies
+        value_copies
+        + first_copies
         + total_copies
         + second_copies
         + forward_copies
@@ -675,6 +732,7 @@
     weight = out_weight.T.reshape(2, columns // 2, FEATS)
     anywhere = pl.BlockSpec(memory_space=pl.ANY)
     dma = pltpu.SemaphoreType.DMA
+    groups = len(GROUPS)
     return pl.pallas_call(
         kernel,
         out_shape=jax.ShapeDtypeStruct((CHUNK, OUTS), BF16),
@@ -684,9 +742,9 @@
             pltpu.VMEM((CHUNKS, CHUNK, FEATS), BF16),
             pltpu.VMEM((CHUNKS * CHUNK, STATE), BF16),
             pltpu.VMEM((CHUNKS * CHUNK, STATE), BF16),
-            pltpu.VMEM((CHUNKS * CHUNK, HEADS_DEV), F32),
+            pltpu.VMEM((HEADS_DEV, CHUNKS * CHUNK), F32),
             pltpu.VMEM((CHUNKS, CHUNK), jnp.int32),
-            pltpu.VMEM((32, 9, HEADS_DEV), F32),
+            pltpu.VMEM((9, HEADS_DEV, 32), F32),
             pltpu.VMEM((1, HEADS_DEV), F32),
             pltpu.VMEM((1, FEATS), F32),
             pltpu.VMEM((4, 4, 2, 80, 2 * FEATS), BF16),
@@ -694,6 +752,8 @@
             pltpu.VMEM((CHUNKS, CHUNK, LANES), F32),
             pltpu.VMEM((16, LANES), F32),
             pltpu.VMEM((CHUNKS, CHUNK, 2 * LANES), BF16),
+            pltpu.VMEM((CHUNKS, 4 * CHUNK, 2 * STATE), BF16),
+            pltpu.VMEM((CHUNKS, CHUNK, 2 * STATE), BF16),
             pltpu.VMEM((16, 8, LANES), F32),
             pltpu.VMEM((32, FEATS), F32),
             pltpu.VMEM((32, FEATS), F32),
@@ -703,15 +763,17 @@
             pltpu.VMEM((CHUNKS, CHUNK, FEATS), F32),
             pltpu.VMEM((4, STATE, FEATS), BF16),
             pltpu.VMEM((4, STATE, FEATS), BF16),
-            pltpu.VMEM((2, STATE, FEATS), BF16),
+            pltpu.VMEM((2, 2 * STATE, FEATS), BF16),
             pltpu.VMEM((4, CHUNK, FEATS), BF16),
             pltpu.VMEM((4, CHUNK, 2 * FEATS), BF16),
             pltpu.VMEM((CHUNK, OUTS), F32),
-            pltpu.VMEM((3, 4, CHUNK, OUTS // 4), BF16),
-            pltpu.VMEM((3, 4, CHUNK, OUTS // 4), BF16),
-            dma((9,)),
-            dma((7,)),
-            dma((7,)),
+            pltpu.VMEM((4, CHUNK, TILE), F32),
+            pltpu.VMEM((3, 4, CHUNK, TILE), BF16),
+            pltpu.VMEM((4, CHUNK, TILE), BF16),
+            pltpu.VMEM((2, 4, CHUNK, TILE), BF16),
+            dma((8,)),
+            dma((groups, 8)),
+            dma((groups, 8)),
             dma((6,)),
             dma((6,)),
             dma((6,)),
@@ -720,14 +782,16 @@
             dma((8,)),
             dma((16,)),
             dma((16,)),
-            dma((3,)),
-            dma((3,)),
-            dma((3,)),
-            dma((3,)),
+            dma((groups, 3)),
+            dma((groups, 3)),
+            dma((groups, 3)),
+            dma((groups, 3)),
             dma((4,)),
             dma((4,)),
-            dma((3, 4)),
-            dma((3, 4)),
+            dma((4,)),
+            dma((4,)),
+            dma((2, 4)),
+            dma((2, 4)),
         ],
         compiler_params=pltpu.CompilerParams(
             collective_id=0,
@@ -739,9 +803,9 @@
         values,
         state_in,
         state_out,
-        log_decay,
+        log_decay.T,
         level_class.reshape(CHUNKS, CHUNK),
-        level_table,
+        level_table.transpose(1, 2, 0),
         skip_gain.reshape(1, -1),
         norm_gain.reshape(1, -1),
         weight,

time: 97.7 us -> 81.8 us (0.84)
  Pallas kernels: 90.6 us -> 78.3 us
  local copies, waits for them, and re-layouts: 6.84 us -> 3.23 us
    pallas_call x1, Pallas kernels: 90.6 us -> 78.3 us  [on_device(): pl.pallas_call(kernel, out_shape=jax.ShapeDtypeStruct((CHUNK, OUTS), BF16...]
    unnamed x3 -> x1, local copies, waits for them, and re-layouts: 5.56 us -> 1.97 us
where the time goes in v1:
time: 81.8 us; the launch traced here: 81.6 us
  Pallas kernels  78.3 us (96%)
  local copies, waits for them, and re-layouts  3.23 us (4%)
    pallas_call x1, Pallas kernels, on_device(): pl.pallas_call(kernel, out_shape=jax.ShapeDtypeStruct((CHUNK, OUTS), BF16...  78.3 us
    unnamed x1, local copies, waits for them, and re-layouts  1.97 us

profile of v1, /device:TPU:1, one launch (start us, length us, event | category | flops | bytes accessed | tf_op | source)
XLA Modules:
  0.0 81.6 jit_solution(3497038442254801490)
XLA Ops:
  0.0 1.3 %reshape.14.norm_gain = f32[1,640]{1,0:T(1,128)} reshape(f32[640]{0:T(1024)} %param.16) | data formatting | bytes 5120 | tf_op jit(solution)/shard_map/reshape | solution.py:810
  1.3 78.3 %layer.1 = bf16[128,2560]{1,0:T(8,128)(2,1)} custom-call(bf16[128,5120]{1,0:T(8,128)(2,1)} %values.1, bf16[1024,128]{1,0:T(8,128)(2,1)} %state_in.1, bf16[1024,128]{1,0:T(8,128)(2,1)} %state_out.1, f32[10,1024]{1,0:T(8,128)} %bitcast.9, s32[8,128]{1,0:T(8,128)} %bitcast.10, f32[9,10,32]{2,1,0:T(8,128)} %bitcast.8, f32[1,10]{1,0:T(1,128)} %bitcast.11, ...), custom_call_target="tpu_custom_call" | custom-call | tf_op jit(solution)/shard_map/layer/pallas_call | solution.py:736
  79.6 2.0 %copy.11 = bf16[128,2560]{1,0:T(8,128)(2,1)} copy(bf16[128,2560]{1,0:T(8,128)(2,1)} %layer.1) | data formatting | bytes 1310720

commit v2 on v1

--- a/solution.py
+++ b/solution.py
@@ -43,6 +43,13 @@
     high = value.astype(BF16)
     low = (value - high.astype(F32)).astype(BF16)
     return jnp.concatenate([high, low], axis=axis)
+
+
+def split3(value):
+    high = value.astype(BF16)
+    rest = value - high.astype(F32)
+    middle = rest.astype(BF16)
+    return high, middle, (rest - middle.astype(F32)).astype(BF16)
 
 
 def kernel(
@@ -146,11 +153,12 @@
         load.start()
     own_lanes = pl.ds(pl.multiple_of(core * FEATS, LANES), FEATS)
     other_lanes = pl.ds(pl.multiple_of((1 - core) * FEATS, LANES), FEATS)
-    for number, (low, high) in enumerate(GROUPS):
+    my_rows = pl.ds(pl.multiple_of(core * CHUNK, CHUNK), CHUNK)
+    for group, (low, high) in enumerate(GROUPS):
         pltpu.make_async_copy(
             values.at[:, pl.ds(pl.multiple_of(head * FEATS + low, LANES), high - low)],
-            rows.at[head, :, low:high],
-            a_recv.at[number, 0],
+            rows.at[y, my_rows, low:high],
+            a_recv.at[group, 0],
         ).start()
     own_weight = pltpu.make_async_copy(
         weight, all_weight.at[z, x, :, :, own_lanes], local_sem.at[7]
@@ -180,21 +188,18 @@
     def near_z(step):
         return lax.rem(z + step, 4) * 4 + x
 
-    def step_of(number):
-        pair = number // 2
-        return pair + (pair // 2) * (1 - 2 * lax.rem(pair, 2)), lax.rem(number, 2)
-
     value_copies = []
     for group, (low, high) in enumerate(GROUPS):
         for number in (6, 7, 2, 3, 4, 5, 1):
-            step_y, step_core = step_of(number)
-            target = lax.rem(y + step_y, 4) * 2 + lax.rem(core + step_core, 2)
+            target = lax.rem(y + (0, 1, 3, 2)[number // 2], 4) * 2 + lax.rem(
+                core + number % 2, 2
+            )
             value_copies.append(
                 copy(
                     values.at[
                         :, pl.ds(pl.multiple_of(target * FEATS + low, LANES), high - low)
                     ],
-                    rows.at[head, :, low:high],
+                    rows.at[y, my_rows, low:high],
                     a_send.at[group, number],
                     a_recv.at[group, number],
                     (ctx, target),
@@ -235,14 +240,17 @@
     causal = (iota((CHUNK, CHUNK), 0) >= iota((CHUNK, CHUNK), 1)) & (
         iota((CHUNK, CHUNK), 0) // 64 == iota((CHUNK, CHUNK), 1) // 64
     )
-    causal_f32 = causal.astype(F32)
+    causal_bf16 = causal.astype(F32).astype(BF16)
+    causal_wide = jnp.concatenate([causal_bf16] * 3, axis=1)
+    spread_bf16 = spread.astype(BF16)
+    within[...] = sum(dot(part, spread_bf16, TN) for part in split3(decay[...]))
     first_half = iota((CHUNK, CHUNK), 1) < 64
 
     @pl.loop(0, CHUNKS)
     def _(j):
         tokens = pl.ds(pl.multiple_of(j * CHUNK, CHUNK), CHUNK)
-        part = exact(causal_f32, exact(decay[:, tokens], spread, TN))
-        within[j] = part
+        part = dot(causal_wide, jnp.concatenate(split3(within[tokens, :]), axis=0))
+        within[tokens, :] = part
         stretch[pl.ds(j * 2, 1), :] = part[63:64, :]
         stretch[pl.ds(j * 2 + 1, 1), :] = part[127:128, :]
 
@@ -262,10 +270,11 @@
         )
         total_copies[-1].start()
 
-    for level in range(10):
-        source = iota((256, FEATS), 0) % LANES
-        target = iota((256, FEATS), 1) // WIDTH + level * HEADS_DEV
-        expander[level] = (source == target).astype(F32).astype(BF16)
+    expander[...] = (
+        (iota((256, FEATS), 0) % LANES == iota((256, FEATS), 1) // WIDTH)
+        .astype(F32)
+        .astype(BF16)
+    )
 
     late = iota((16, 16), 0)
     early = iota((16, 16), 1)
@@ -289,8 +298,56 @@
     )
     pick = pick | ((block == 22) & (piece >= 8))
     row_factors[...] = dot(
-        split(jnp.exp(exact(pick.astype(F32), sums))), expander[0]
+        split(jnp.exp(exact(pick.astype(F32), sums))), expander[...]
     )
+
+    own_weight.wait()
+    for item in first_copies:
+        item.wait_recv()
+    above_z = lax.rem(z + 1, 4)
+    below_z = lax.rem(z + 3, 4)
+    far_z = lax.rem(z + 2, 4)
+    above_x = lax.rem(x + 1, 4)
+    below_x = lax.rem(x + 3, 4)
+    far_x = lax.rem(x + 2, 4)
+    slabs = [
+        lambda lanes: all_weight.at[z, :, 0, :, lanes],
+        lambda lanes: all_weight.at[:, x, 1, :, lanes],
+        lambda lanes: all_weight.at[below_z, :, 0, :, lanes],
+        lambda lanes: all_weight.at[above_z, :, 0, :, lanes],
+        lambda lanes: all_weight.at[:, below_x, 1, :, lanes],
+        lambda lanes: all_weight.at[:, above_x, 1, :, lanes],
+        lambda lanes: all_weight.at[far_z, 0:2, 0, :, lanes],
+        lambda lanes: all_weight.at[far_z, 2:4, 0, :, lanes],
+        lambda lanes: all_weight.at[0:2, far_x, 1, :, lanes],
+        lambda lanes: all_weight.at[2:4, far_x, 1, :, lanes],
+    ]
+    second_copies = []
+    forward_copies = []
+
+    def pass_on(part, number, device):
+        item = copy(part, part, w2_send.at[number], w2_recv.at[number], (device, head))
+        item.start()
+        second_copies.append(item)
+
+    def arrived(number):
+        part = slabs[number + 2](own_lanes)
+        copy(
+            part, part, w2_send.at[number], w2_recv.at[number], (near_z(1), head)
+        ).wait_recv()
+
+    def forward(number):
+        part = slabs[number](own_lanes)
+        item = copy(part, part, wf_send.at[number], wf_recv.at[number], (ctx, partner))
+        item.start()
+        forward_copies.append(item)
+
+    pass_on(slabs[0](own_lanes), 0, near_z(1))
+    pass_on(slabs[0](own_lanes), 1, near_z(3))
+    pass_on(slabs[1](own_lanes), 2, near_x(1))
+    pass_on(slabs[1](own_lanes), 3, near_x(3))
+    forward(0)
+    forward(1)
 
     table_rows = jnp.zeros((32, LANES), F32)
     for level in range(9):
@@ -299,15 +356,17 @@
             jnp.where(iota((HEADS_DEV, LANES), 1) // HEADS_DEV == level, spread, 0.0),
             TN,
         )
+    table_wide = jnp.concatenate(split3(table_rows), axis=0)
     class_rows = iota((32, CHUNK), 0)
     lift_lane = (lane_level == LIFT).astype(F32)
     second_row = iota((CHUNK, LANES), 0) // 64
 
     @pl.loop(0, CHUNKS)
     def _(j):
-        onehot = (class_rows == classes[pl.ds(j, 1), :]).astype(F32)
-        weights = exact(onehot, table_rows, TN) + lift_lane
-        part = within[j]
+        tokens = pl.ds(pl.multiple_of(j * CHUNK, CHUNK), CHUNK)
+        onehot = (class_rows == classes[pl.ds(j, 1), :]).astype(F32).astype(BF16)
+        weights = dot(jnp.concatenate([onehot] * 3, axis=0), table_wide, TN) + lift_lane
+        part = within[tokens, :]
         start = jnp.where(
             second_row == 0, stretch[pl.ds(j * 2, 1), :], stretch[pl.ds(j * 2 + 1, 1), :]
         )
@@ -325,11 +384,13 @@
                 ),
             ),
         )
-        factors[j] = split(jnp.where(bit == 1, jnp.exp(exponent) * weights, 0.0))
-        tokens = pl.ds(pl.multiple_of(j * CHUNK, CHUNK), CHUNK)
+        every = jnp.where(bit == 1, jnp.exp(exponent) * weights, 0.0)
+        for level in range(10):
+            turn = (LANES - level * HEADS_DEV) % LANES
+            factors[level, tokens, :] = split(pltpu.roll(every, turn, 1) if turn else every)
         incoming = entering[tokens, :]
         reader = leaving[tokens, :]
-        readers[j] = jnp.concatenate([reader, reader], axis=1)
+        readers[tokens, :] = jnp.concatenate([reader, reader], axis=1)
         scores = jnp.where(causal, dot(reader, incoming, NT), 0.0)
         score_high = scores.astype(BF16)
         score_low = (scores - score_high.astype(F32)).astype(BF16)
@@ -339,85 +400,58 @@
         half = jnp.concatenate([score_high, score_low, lower, upper], axis=0)
         mixers[j] = jnp.concatenate([half, half], axis=1)
 
-    skip_row = dot(split(exact(skip[...], spread)), expander[0])
-
-    own_weight.wait()
-    for item in first_copies:
-        item.wait_recv()
-    second_copies = []
-    forward_copies = []
-    for number, step in enumerate((2, 1, 3)):
-        second_copies.append(
-            copy(
-                all_weight.at[z, :, 0, :, own_lanes],
-                all_weight.at[z, :, 0, :, own_lanes],
-                w2_send.at[number],
-                w2_recv.at[number],
-                (near_z(step), head),
-            )
-        )
-        second_copies.append(
-            copy(
-                all_weight.at[:, x, 1, :, own_lanes],
-                all_weight.at[:, x, 1, :, own_lanes],
-                w2_send.at[3 + number],
-                w2_recv.at[3 + number],
-                (near_x(step), head),
-            )
-        )
-    for item in second_copies:
-        item.start()
-
-    def forward(slab, number):
-        item = copy(
-            slab(own_lanes),
-            slab(own_lanes),
-            wf_send.at[number],
-            wf_recv.at[number],
-            (ctx, partner),
-        )
-        item.start()
-        forward_copies.append(item)
-
-    forward(lambda lanes: all_weight.at[z, :, 0, :, lanes], 0)
-    forward(lambda lanes: all_weight.at[:, x, 1, :, lanes], 1)
-
-    def chunk_work(j, low, high):
-        inputs = rows[j, :, low:high].astype(F32)
-        factor = factors[j]
-        lifted = split(dot(factor, expander[LIFT, :, low:high]) * inputs, 0)
-        product = dot(mixers[j], lifted)
-        lower_state = row_factors[pl.ds(j * 2, 1), low:high] * product[256:384]
-        pair_state[j, :, low:high] = row_factors[pl.ds(j * 2 + 1, 1), low:high] * (
-            lower_state + product[384:512]
-        )
-        gained = dot(readers[j], split(lower_state, 0))
-        output[j, :, low:high] = (
-            dot(factor, expander[0, :, low:high]) * (product[:128] + product[128:256])
-            + dot(factor, expander[1, :, low:high]) * gained
-            + skip_row[:, low:high] * inputs
+    skip_row = dot(split(exact(skip[...], spread)), expander[...])
+
+    def pair_work(pair, low, high):
+        inputs = rows[pair, :, low:high].astype(F32)
+        tokens = pl.ds(pl.multiple_of(pair * 256, 256), 256)
+        expanded = dot(
+            jnp.concatenate(
+                [factors[LIFT, tokens, :], factors[0, tokens, :], factors[1, tokens, :]],
+                axis=0,
+            ),
+            expander[:, low:high],
+        )
+        lifted = expanded[:256] * inputs
+        states = []
+        for half in range(2):
+            start = half * CHUNK
+            part = slice(start, start + CHUNK)
+            j = pair * 2 + half
+            product = dot(mixers[j], split(lifted[part], 0))
+            lower_state = row_factors[pl.ds(j * 2, 1), low:high] * product[256:384]
+            states.append(
+                row_factors[pl.ds(j * 2 + 1, 1), low:high]
+                * (lower_state + product[384:512])
+            )
+            gained = dot(
+                readers[pl.ds(pl.multiple_of(j * CHUNK, CHUNK), CHUNK), :],
+                split(lower_state, 0),
+            )
+            output[pair, part, low:high] = (
+                expanded[256 + start : 384 + start] * (product[:128] + product[128:256])
+                + expanded[512 + start : 640 + start] * gained
+                + skip_row[:, low:high] * inputs[part]
+            )
+        pair_state[pair, :, low:high] = states[0]
+        quad_state[pair, :, low:high] = (
+            row_factors[pl.ds(16 + pair, 1), low:high] * states[0] + states[1]
         )
 
     x_copies = []
     for group, (low, high) in enumerate(GROUPS):
 
-        @pl.loop(0, CHUNKS)
-        def _(number):
-            step_y, step_core = step_of(number)
-            origin = lax.rem(y + 4 - step_y, 4) * 2 + lax.rem(core + 2 - step_core, 2)
-            pltpu.make_async_copy(
-                rows.at[origin, :, low:high],
-                rows.at[origin, :, low:high],
-                a_recv.at[group, number],
-            ).wait()
-            chunk_work(origin, low, high)
-
-        for quad in range(4):
-            quad_state[quad, :, low:high] = (
-                row_factors[16 + quad : 17 + quad, low:high]
-                * pair_state[2 * quad, :, low:high]
-                + pair_state[2 * quad + 1, :, low:high]
-            )
+        @pl.loop(0, 4)
+        def _(order):
+            step = order + (order // 2) * (1 - 2 * lax.rem(order, 2))
+            pair = lax.rem(y + 4 - step, 4)
+            for half in range(2):
+                place = rows.at[pair, half * CHUNK : (half + 1) * CHUNK, low:high]
+                pltpu.make_async_copy(
+                    place, place, a_recv.at[group, order * 2 + half]
+                ).wait()
+            pair_work(pair, low, high)
+
         for half in range(2):
             half_state[half, :, low:high] = (
                 row_factors[20 + half : 21 + half, low:high]
@@ -470,7 +504,7 @@
             used = used | ((kind == 3) & (slot == z - 1) & (lax.rem(z, 2) == 1))
             used = used | ((kind == 4) & (z >= 2) & (slot < 2))
             mix = jnp.where(used, jnp.exp(exact(counted.astype(F32), every_total)), 0.0)
-            mix_factors[...] = dot(split(mix), expander[0])
+            mix_factors[...] = dot(split(mix), expander[...])
 
     def mixed(ring, start, low, high):
         total = jnp.zeros((STATE, high - low), F32)
@@ -491,20 +525,46 @@
                 (device(origin), head),
             ).wait_recv()
 
-    def read_local(group):
-        for level in (2, 3, 4):
-            if level == 2:
-                j = group * 2 + 1
-                state = pair_state[group * 2]
-            elif level == 3:
-                j = 2 + lax.rem(group, 2) + 4 * (group // 2)
-                state = quad_state[(group // 2) * 2]
-            else:
-                j = 4 + group
-                state = half_state[0]
-            output[j] = output[j] + dot(factors[j], expander[level]) * dot(
-                readers[j], split(state, 0)
-            )
+    def read_local(step):
+        def rows_of(start, count):
+            return pl.ds(pl.multiple_of(start, CHUNK), count)
+
+        first = rows_of(step * 512 + 128, 128)
+        second = rows_of(step * 512 + 384, 128)
+        third = rows_of(step * 512 + 256, 256)
+        fourth = rows_of(512 + step * 256, 256)
+        expanded = dot(
+            jnp.concatenate(
+                [
+                    factors[2, first, :],
+                    factors[2, second, :],
+                    factors[3, third, :],
+                    factors[4, fourth, :],
+                ],
+                axis=0,
+            ),
+            expander[...],
+        )
+        upper = slice(CHUNK, 2 * CHUNK)
+        output[step * 2, upper, :] += expanded[:128] * dot(
+            readers[first, :], split(pair_state[step * 2], 0)
+        )
+        output[step * 2 + 1, upper, :] += expanded[128:256] * dot(
+            readers[second, :], split(pair_state[step * 2 + 1], 0)
+        )
+        output[step * 2 + 1] += expanded[256:512] * dot(
+            readers[third, :], split(quad_state[step * 2], 0)
+        )
+        output[2 + step] += expanded[512:] * dot(
+            readers[fourth, :], split(half_state[0], 0)
+        )
+
+    arrived(0)
+    arrived(1)
+    pass_on(all_weight.at[below_z, 0:2, 0, :, own_lanes], 4, near_z(1))
+    pass_on(all_weight.at[above_z, 2:4, 0, :, own_lanes], 5, near_z(3))
+    forward(2)
+    forward(3)
 
     z_copies = []
     for group, (low, high) in enumerate(GROUPS):
@@ -524,38 +584,33 @@
         buckets[0, :, low:high] = split(mixed(ring_x, 0, low, high), 0)
         buckets[1, :, low:high] = split(mixed(ring_x, 4, low, high), 0)
         if group == 0:
-            pl.loop(0, 4)(read_local)
-
-    def read_levels(j, low):
-        factor = factors[j]
-        reader = readers[j]
-        return dot(factor, expander[low]) * dot(reader, buckets[0]) + dot(
-            factor, expander[low + 1]
-        ) * dot(reader, buckets[1])
-
-    @pl.loop(0, CHUNKS)
-    def _(j):
-        output[j] = output[j] + read_levels(j, 5)
-
-    for number, step in enumerate((2, 1, 3)):
-        from_z = lax.rem(z + 4 - step, 4)
-        copy(
-            all_weight.at[from_z, :, 0, :, own_lanes],
-            all_weight.at[from_z, :, 0, :, own_lanes],
-            w2_send.at[number],
-            w2_recv.at[number],
-            (from_z * 4 + x, head),
-        ).wait_recv()
-        forward(lambda lanes: all_weight.at[from_z, :, 0, :, lanes], 2 + number)
-        from_x = lax.rem(x + 4 - step, 4)
-        copy(
-            all_weight.at[:, from_x, 1, :, own_lanes],
-            all_weight.at[:, from_x, 1, :, own_lanes],
-            w2_send.at[3 + number],
-            w2_recv.at[3 + number],
-            (z * 4 + from_x, head),
-        ).wait_recv()
-        forward(lambda lanes: all_weight.at[:, from_x, 1, :, lanes], 5 + number)
+            pl.loop(0, 2)(read_local)
+
+    arrived(2)
+    arrived(3)
+    pass_on(all_weight.at[0:2, below_x, 1, :, own_lanes], 6, near_x(1))
+    pass_on(all_weight.at[2:4, above_x, 1, :, own_lanes], 7, near_x(3))
+    forward(4)
+    forward(5)
+
+    def read_levels(start, count, low):
+        tokens = pl.ds(pl.multiple_of(start, CHUNK), count)
+        reader = readers[tokens, :]
+        expanded = dot(
+            jnp.concatenate([factors[low, tokens, :], factors[low + 1, tokens, :]], axis=0),
+            expander[...],
+        )
+        return expanded[:count] * dot(reader, buckets[0]) + expanded[count:] * dot(
+            reader, buckets[1]
+        )
+
+    @pl.loop(0, 4)
+    def _(pair):
+        output[pair] = output[pair] + read_levels(pair * 256, 256, 5)
+
+    for number in (4, 5, 6, 7):
+        arrived(number)
+        forward(number + 2)
 
     for group, (low, high) in enumerate(GROUPS):
         hear(ring_z, z_recv, group, low, high, z, lambda origin: origin * 4 + x)
@@ -566,14 +621,17 @@
         iota((256, LANES), 0) % LANES // WIDTH == iota((256, LANES), 1) // WIDTH
     ).astype(F32).astype(BF16)
 
-    def finish(j):
-        total = output[j] + read_levels(j, 7)
+    gain_row = gain[...].reshape(1, FEATS)
+
+    def finish(pair, side):
+        here = pl.ds(pl.multiple_of(side * CHUNK, CHUNK), CHUNK)
+        total = output[pair, here, :] + read_levels(pair * 256 + side * CHUNK, CHUNK, 7)
         pieces = []
         for group in range(FEATS // LANES):
             part = total[:, group * LANES : (group + 1) * LANES]
             mean_square = dot(split(part * part), same_head) * (1.0 / WIDTH)
             scaled = part * lax.rsqrt(mean_square + EPSILON)
-            pieces.append(scaled * gain[:, group * LANES : (group + 1) * LANES])
+            pieces.append(scaled * gain_row[:, group * LANES : (group + 1) * LANES])
         return jnp.concatenate(pieces, axis=1).astype(BF16)
 
     def place_chip(place):
@@ -582,7 +640,7 @@
     normed_copies = []
 
     def hand_over(place):
-        normed_send[place] = finish(place_chip(place) * 2 + (1 - core))
+        normed_send[place] = finish(place_chip(place), 1 - core)
         normed_copies.append(
             copy(
                 normed_send.at[place],
@@ -595,21 +653,11 @@
         normed_copies[-1].start()
 
     def keep(place):
-        normed_all[place, :, own_lanes] = finish(place_chip(place) * 2 + core)
+        normed_all[place, :, own_lanes] = finish(place_chip(place), core)
 
     hand_over(0)
     keep(0)
     hand_over(1)
-    slabs = [
-        lambda lanes: all_weight.at[z, :, 0, :, lanes],
-        lambda lanes: all_weight.at[:, x, 1, :, lanes],
-    ]
-    for number, step in enumerate((2, 1, 3)):
-        from_z = lax.rem(z + 4 - step, 4)
-        slabs.append(lambda lanes, at=from_z: all_weight.at[at, :, 0, :, lanes])
-    for number, step in enumerate((2, 1, 3)):
-        from_x = lax.rem(x + 4 - step, 4)
-        slabs.append(lambda lanes, at=from_x: all_weight.at[:, at, 1, :, lanes])
     for number, slab in enumerate(slabs):
         copy(
             slab(other_lanes),
@@ -739,28 +787,28 @@
         in_specs=[anywhere] * 9,
         out_specs=pl.BlockSpec(memory_space=pltpu.VMEM),
         scratch_shapes=[
-            pltpu.VMEM((CHUNKS, CHUNK, FEATS), BF16),
+            pltpu.VMEM((4, 2 * CHUNK, FEATS), BF16),
             pltpu.VMEM((CHUNKS * CHUNK, STATE), BF16),
             pltpu.VMEM((CHUNKS * CHUNK, STATE), BF16),
             pltpu.VMEM((HEADS_DEV, CHUNKS * CHUNK), F32),
             pltpu.VMEM((CHUNKS, CHUNK), jnp.int32),
             pltpu.VMEM((9, HEADS_DEV, 32), F32),
             pltpu.VMEM((1, HEADS_DEV), F32),
-            pltpu.VMEM((1, FEATS), F32),
+            pltpu.VMEM((FEATS,), F32),
             pltpu.VMEM((4, 4, 2, 80, 2 * FEATS), BF16),
-            pltpu.VMEM((10, 256, FEATS), BF16),
-            pltpu.VMEM((CHUNKS, CHUNK, LANES), F32),
+            pltpu.VMEM((256, FEATS), BF16),
+            pltpu.VMEM((CHUNKS * CHUNK, LANES), F32),
             pltpu.VMEM((16, LANES), F32),
-            pltpu.VMEM((CHUNKS, CHUNK, 2 * LANES), BF16),
+            pltpu.VMEM((10, CHUNKS * CHUNK, 2 * LANES), BF16),
             pltpu.VMEM((CHUNKS, 4 * CHUNK, 2 * STATE), BF16),
-            pltpu.VMEM((CHUNKS, CHUNK, 2 * STATE), BF16),
+            pltpu.VMEM((CHUNKS * CHUNK, 2 * STATE), BF16),
             pltpu.VMEM((16, 8, LANES), F32),
             pltpu.VMEM((32, FEATS), F32),
             pltpu.VMEM((32, FEATS), F32),
-            pltpu.VMEM((CHUNKS, STATE, FEATS), F32),
+            pltpu.VMEM((4, STATE, FEATS), F32),
             pltpu.VMEM((4, STATE, FEATS), F32),
             pltpu.VMEM((2, STATE, FEATS), F32),
-            pltpu.VMEM((CHUNKS, CHUNK, FEATS), F32),
+            pltpu.VMEM((4, 2 * CHUNK, FEATS), F32),
             pltpu.VMEM((4, STATE, FEATS), BF16),
             pltpu.VMEM((4, STATE, FEATS), BF16),
             pltpu.VMEM((2, 2 * STATE, FEATS), BF16),
@@ -776,10 +824,10 @@
             dma((groups, 8)),
             dma((6,)),
             dma((6,)),
-            dma((6,)),
-            dma((6,)),
             dma((8,)),
             dma((8,)),
+            dma((10,)),
+            dma((10,)),
             dma((16,)),
             dma((16,)),
             dma((groups, 3)),
@@ -807,7 +855,7 @@
         level_class.reshape(CHUNKS, CHUNK),
         level_table.transpose(1, 2, 0),
         skip_gain.reshape(1, -1),
-        norm_gain.reshape(1, -1),
+        norm_gain,
         weight,
     )
 

time: 81.8 us -> 72.2 us (0.88)
  Pallas kernels: 78.3 us -> 70.1 us
  local copies, waits for them, and re-layouts: 3.23 us -> 1.97 us
    pallas_call x1, Pallas kernels: 78.3 us -> 70.1 us  [on_device(): pl.pallas_call(kernel, out_shape=jax.ShapeDtypeStruct((CHUNK, OUTS), BF16...]
    reshape x1 -> x0, local copies, waits for them, and re-layouts: 1.27 us -> none  [on_device(): norm_gain.reshape(1, -1)]
where the time goes in v2:
time: 72.2 us; the launch traced here: 72.1 us
  Pallas kernels  70.1 us (97%)
  local copies, waits for them, and re-layouts  1.97 us (3%)
    pallas_call x1, Pallas kernels, on_device(): pl.pallas_call(kernel, out_shape=jax.ShapeDtypeStruct((CHUNK, OUTS), BF16...  70.1 us
    unnamed x1, local copies, waits for them, and re-layouts  1.97 us

profile of v2, /device:TPU:1, one launch (start us, length us, event | category | flops | bytes accessed | tf_op | source)
XLA Modules:
  0.0 72.1 jit_solution(3431821498475379035)
XLA Ops:
  0.0 70.1 %layer.1 = bf16[128,2560]{1,0:T(8,128)(2,1)} custom-call(bf16[128,5120]{1,0:T(8,128)(2,1)} %values.1, bf16[1024,128]{1,0:T(8,128)(2,1)} %state_in.1, bf16[1024,128]{1,0:T(8,128)(2,1)} %state_out.1, f32[10,1024]{1,0:T(8,128)} %bitcast.9, s32[8,128]{1,0:T(8,128)} %bitcast.10, f32[9,10,32]{2,1,0:T(8,128)} %bitcast.8, f32[1,10]{1,0:T(1,128)} %bitcast.11, ...), custom_call_target="tpu_custom_call" | custom-call | tf_op jit(solution)/shard_map/layer/pallas_call | solution.py:784
  70.1 2.0 %copy.11 = bf16[128,2560]{1,0:T(8,128)(2,1)} copy(bf16[128,2560]{1,0:T(8,128)(2,1)} %layer.1) | data formatting | bytes 1310720

commit v3 on v2

--- a/solution.py
+++ b/solution.py
@@ -173,20 +173,18 @@
             device_id=(ctx, lax.rem(head + step, 8)),
             device_id_type=MESH,
         )
-    for step in range(1, 16):
-        pl.semaphore_signal(
-            barrier,
-            inc=1,
-            device_id=(lax.rem(ctx + step, 16), head),
-            device_id_type=MESH,
-        )
-    pl.semaphore_wait(barrier, 22)
-
     def near_x(step):
         return z * 4 + lax.rem(x + step, 4)
 
     def near_z(step):
         return lax.rem(z + step, 4) * 4 + x
+
+    for step in range(1, 4):
+        for device in (near_x(step), near_z(step)):
+            pl.semaphore_signal(
+                barrier, inc=1, device_id=(device, head), device_id_type=MESH
+            )
+    pl.semaphore_wait(barrier, 13)
 
     value_copies = []
     for group, (low, high) in enumerate(GROUPS):
@@ -256,19 +254,33 @@
 
     sums = stretch[...]
     total_row = jnp.sum(sums, axis=0, keepdims=True)
-    totals[ctx] = jnp.broadcast_to(total_row, (8, LANES))
+    totals[z, x] = jnp.broadcast_to(total_row, (8, LANES))
     total_copies = []
-    for step in range(1, 16):
-        total_copies.append(
+
+    def share_totals(part, first, device):
+        for step in range(1, 4):
+            item = copy(
+                part,
+                part,
+                t_send.at[first + step],
+                t_recv.at[first + step],
+                (device(step), head),
+            )
+            item.start()
+            total_copies.append(item)
+
+    def hear_totals(part, first):
+        for step in range(1, 4):
+            piece = part(step)
             copy(
-                totals.at[ctx],
-                totals.at[ctx],
-                t_send.at[step],
-                t_recv.at[step],
-                (lax.rem(ctx + step, 16), head),
-            )
-        )
-        total_copies[-1].start()
+                piece,
+                piece,
+                t_send.at[first + step],
+                t_recv.at[first + step],
+                (near_x(1), head),
+            ).wait_recv()
+
+    share_totals(totals.at[z, x], 0, near_x)
 
     expander[...] = (
         (iota((256, FEATS), 0) % LANES == iota((256, FEATS), 1) // WIDTH)
@@ -300,6 +312,62 @@
     row_factors[...] = dot(
         split(jnp.exp(exact(pick.astype(F32), sums))), expander[...]
     )
+
+    table_rows = jnp.zeros((32, LANES), F32)
+    for level in range(9):
+        table_rows = table_rows + exact(
+            table[level],
+            jnp.where(iota((HEADS_DEV, LANES), 1) // HEADS_DEV == level, spread, 0.0),
+            TN,
+        )
+    table_wide = jnp.concatenate(split3(table_rows), axis=0)
+    class_rows = iota((32, CHUNK), 0)
+    lift_lane = (lane_level == LIFT).astype(F32)
+    second_row = iota((CHUNK, LANES), 0) // 64
+
+    @pl.loop(0, CHUNKS)
+    def _(j):
+        tokens = pl.ds(pl.multiple_of(j * CHUNK, CHUNK), CHUNK)
+        onehot = (class_rows == classes[pl.ds(j, 1), :]).astype(F32).astype(BF16)
+        weights = dot(jnp.concatenate([onehot] * 3, axis=0), table_wide, TN) + lift_lane
+        part = within[tokens, :]
+        start = jnp.where(
+            second_row == 0, stretch[pl.ds(j * 2, 1), :], stretch[pl.ds(j * 2 + 1, 1), :]
+        )
+        exponent = jnp.where(lane_level == LIFT, -part, part + start)
+        bit = jnp.where(
+            lane_level == 1,
+            second_row,
+            jnp.where(
+                lane_level == 2,
+                lax.rem(j, 2),
+                jnp.where(
+                    lane_level == 3,
+                    lax.rem(j // 2, 2),
+                    jnp.where(lane_level == 4, j // 4, 1),
+                ),
+            ),
+        )
+        every = jnp.where(bit == 1, jnp.exp(exponent) * weights, 0.0)
+        for level in range(10):
+            turn = (LANES - level * HEADS_DEV) % LANES
+            factors[level, tokens, :] = split(pltpu.roll(every, turn, 1) if turn else every)
+        incoming = entering[tokens, :]
+        reader = leaving[tokens, :]
+        readers[tokens, :] = jnp.concatenate([reader, reader], axis=1)
+        scores = jnp.where(causal, dot(reader, incoming, NT), 0.0)
+        score_high = scores.astype(BF16)
+        score_low = (scores - score_high.astype(F32)).astype(BF16)
+        turned = incoming.astype(F32).T
+        lower = jnp.where(first_half, turned, 0.0).astype(BF16)
+        upper = jnp.where(first_half, 0.0, turned).astype(BF16)
+        half = jnp.concatenate([score_high, score_low, lower, upper], axis=0)
+        mixers[j] = jnp.concatenate([half, half], axis=1)
+
+    skip_row = dot(split(exact(skip[...], spread)), expander[...])
+
+    hear_totals(lambda step: totals.at[z, lax.rem(x + 4 - step, 4)], 0)
+    share_totals(totals.at[z], 4, near_z)
 
     own_weight.wait()
     for item in first_copies:
@@ -349,59 +417,6 @@
     forward(0)
     forward(1)
 
-    table_rows = jnp.zeros((32, LANES), F32)
-    for level in range(9):
-        table_rows = table_rows + exact(
-            table[level],
-            jnp.where(iota((HEADS_DEV, LANES), 1) // HEADS_DEV == level, spread, 0.0),
-            TN,
-        )
-    table_wide = jnp.concatenate(split3(table_rows), axis=0)
-    class_rows = iota((32, CHUNK), 0)
-    lift_lane = (lane_level == LIFT).astype(F32)
-    second_row = iota((CHUNK, LANES), 0) // 64
-
-    @pl.loop(0, CHUNKS)
-    def _(j):
-        tokens = pl.ds(pl.multiple_of(j * CHUNK, CHUNK), CHUNK)
-        onehot = (class_rows == classes[pl.ds(j, 1), :]).astype(F32).astype(BF16)
-        weights = dot(jnp.concatenate([onehot] * 3, axis=0), table_wide, TN) + lift_lane
-        part = within[tokens, :]
-        start = jnp.where(
-            second_row == 0, stretch[pl.ds(j * 2, 1), :], stretch[pl.ds(j * 2 + 1, 1), :]
-        )
-        exponent = jnp.where(lane_level == LIFT, -part, part + start)
-        bit = jnp.where(
-            lane_level == 1,
-            second_row,
-            jnp.where(
-                lane_level == 2,
-                lax.rem(j, 2),
-                jnp.where(
-                    lane_level == 3,
-                    lax.rem(j // 2, 2),
-                    jnp.where(lane_level == 4, j // 4, 1),
-                ),
-            ),
-        )
-        every = jnp.where(bit == 1, jnp.exp(exponent) * weights, 0.0)
-        for level in range(10):
-            turn = (LANES - level * HEADS_DEV) % LANES
-            factors[level, tokens, :] = split(pltpu.roll(every, turn, 1) if turn else every)
-        incoming = entering[tokens, :]
-        reader = leaving[tokens, :]
-        readers[tokens, :] = jnp.concatenate([reader, reader], axis=1)
-        scores = jnp.where(causal, dot(reader, incoming, NT), 0.0)
-        score_high = scores.astype(BF16)
-        score_low = (scores - score_high.astype(F32)).astype(BF16)
-        turned = incoming.astype(F32).T
-        lower = jnp.where(first_half, turned, 0.0).astype(BF16)
-        upper = jnp.where(first_half, 0.0, turned).astype(BF16)
-        half = jnp.concatenate([score_high, score_low, lower, upper], axis=0)
-        mixers[j] = jnp.concatenate([half, half], axis=1)
-
-    skip_row = dot(split(exact(skip[...], spread)), expander[...])
-
     def pair_work(pair, low, high):
         inputs = rows[pair, :, low:high].astype(F32)
         tokens = pl.ds(pl.multiple_of(pair * 256, 256), 256)
@@ -419,9 +434,9 @@
             part = slice(start, start + CHUNK)
             j = pair * 2 + half
             product = dot(mixers[j], split(lifted[part], 0))
-            lower_state = row_factors[pl.ds(j * 2, 1), low:high] * product[256:384]
+            lower_state = row_factors[pl.ds(j * 2, 1), :][:, low:high] * product[256:384]
             states.append(
-                row_factors[pl.ds(j * 2 + 1, 1), low:high]
+                row_factors[pl.ds(j * 2 + 1, 1), :][:, low:high]
                 * (lower_state + product[384:512])
             )
             gained = dot(
@@ -435,7 +450,7 @@
             )
         pair_state[pair, :, low:high] = states[0]
         quad_state[pair, :, low:high] = (
-            row_factors[pl.ds(16 + pair, 1), low:high] * states[0] + states[1]
+            row_factors[pl.ds(16 + pair, 1), :][:, low:high] * states[0] + states[1]
         )
 
     x_copies = []
@@ -474,16 +489,10 @@
             )
             x_copies[-1].start()
         if group == 0:
-            for step in range(1, 16):
-                origin = lax.rem(ctx + 16 - step, 16)
-                copy(
-                    totals.at[origin],
-                    totals.at[origin],
-                    t_send.at[step],
-                    t_recv.at[step],
-                    (origin, head),
-                ).wait_recv()
-            every_total = jnp.concatenate([totals[d][0:1, :] for d in range(16)], axis=0)
+            hear_totals(lambda step: totals.at[lax.rem(z + 4 - step, 4)], 4)
+            every_total = jnp.concatenate(
+                [totals[d // 4, d % 4][0:1, :] for d in range(16)], axis=0
+            )
             row = iota((32, 16), 0)
             shard = iota((32, 16), 1)
             kind = row // 4
@@ -565,6 +574,7 @@
     pass_on(all_weight.at[above_z, 2:4, 0, :, own_lanes], 5, near_z(3))
     forward(2)
     forward(3)
+    pl.loop(0, 2)(read_local)
 
     z_copies = []
     for group, (low, high) in enumerate(GROUPS):
@@ -583,8 +593,6 @@
             z_copies[-1].start()
         buckets[0, :, low:high] = split(mixed(ring_x, 0, low, high), 0)
         buckets[1, :, low:high] = split(mixed(ring_x, 4, low, high), 0)
-        if group == 0:
-            pl.loop(0, 2)(read_local)
 
     arrived(2)
     arrived(3)
@@ -802,7 +810,7 @@
             pltpu.VMEM((10, CHUNKS * CHUNK, 2 * LANES), BF16),
             pltpu.VMEM((CHUNKS, 4 * CHUNK, 2 * STATE), BF16),
             pltpu.VMEM((CHUNKS * CHUNK, 2 * STATE), BF16),
-            pltpu.VMEM((16, 8, LANES), F32),
+            pltpu.VMEM((4, 4, 8, LANES), F32),
             pltpu.VMEM((32, FEATS), F32),
             pltpu.VMEM((32, FEATS), F32),
             pltpu.VMEM((4, STATE, FEATS), F32),
@@ -828,8 +836,8 @@
             dma((8,)),
             dma((10,)),
             dma((10,)),
-            dma((16,)),
-            dma((16,)),
+            dma((8,)),
+            dma((8,)),
             dma((groups, 3)),
             dma((groups, 3)),
             dma((groups, 3)),

time: 72.2 us -> 70.7 us (0.979)
  Pallas kernels: 70.1 us -> 68.6 us
    pallas_call x1, Pallas kernels: 70.1 us -> 68.6 us  [on_device(): pl.pallas_call(kernel, out_shape=jax.ShapeDtypeStruct((CHUNK, OUTS), BF16...]
where the time goes in v3:
time: 70.7 us; the launch traced here: 70.5 us
  Pallas kernels  68.6 us (97%)
  local copies, waits for them, and re-layouts  1.97 us (3%)
    pallas_call x1, Pallas kernels, on_device(): pl.pallas_call(kernel, out_shape=jax.ShapeDtypeStruct((CHUNK, OUTS), BF16...  68.6 us
    unnamed x1, local copies, waits for them, and re-layouts  1.97 us

profile of v3, /device:TPU:1, one launch (start us, length us, event | category | flops | bytes accessed | tf_op | source)
XLA Modules:
  0.0 70.5 jit_solution(4021941438631242377)
XLA Ops:
  0.0 68.6 %layer.1 = bf16[128,2560]{1,0:T(8,128)(2,1)} custom-call(bf16[128,5120]{1,0:T(8,128)(2,1)} %values.1, bf16[1024,128]{1,0:T(8,128)(2,1)} %state_in.1, bf16[1024,128]{1,0:T(8,128)(2,1)} %state_out.1, f32[10,1024]{1,0:T(8,128)} %bitcast.9, s32[8,128]{1,0:T(8,128)} %bitcast.10, f32[9,10,32]{2,1,0:T(8,128)} %bitcast.8, f32[1,10]{1,0:T(1,128)} %bitcast.11, ...), custom_call_target="tpu_custom_call" | custom-call | tf_op jit(solution)/shard_map/layer/pallas_call | solution.py:792
  68.6 2.0 %copy.11 = bf16[128,2560]{1,0:T(8,128)(2,1)} copy(bf16[128,2560]{1,0:T(8,128)(2,1)} %layer.1) | data formatting | bytes 1310720

commit v4 on v3

--- a/solution.py
+++ b/solution.py
@@ -91,6 +91,7 @@
     normed_send,
     normed_all,
     own_sum,
+    rounded,
     held,
     partial_send,
     relay_recv,
@@ -135,6 +136,26 @@
             device_id_type=MESH,
         )
 
+    barrier = pltpu.get_barrier_semaphore()
+    for step in range(1, 8):
+        pl.semaphore_signal(
+            barrier,
+            inc=1,
+            device_id=(ctx, lax.rem(head + step, 8)),
+            device_id_type=MESH,
+        )
+    def near_x(step):
+        return z * 4 + lax.rem(x + step, 4)
+
+    def near_z(step):
+        return lax.rem(z + step, 4) * 4 + x
+
+    for step in range(1, 4):
+        for device in (near_x(step), near_z(step)):
+            pl.semaphore_signal(
+                barrier, inc=1, device_id=(device, head), device_id_type=MESH
+            )
+
     loads = [
         pltpu.make_async_copy(source, target, local_sem.at[number])
         for number, (source, target) in enumerate(
@@ -165,25 +186,6 @@
     )
     own_weight.start()
 
-    barrier = pltpu.get_barrier_semaphore()
-    for step in range(1, 8):
-        pl.semaphore_signal(
-            barrier,
-            inc=1,
-            device_id=(ctx, lax.rem(head + step, 8)),
-            device_id_type=MESH,
-        )
-    def near_x(step):
-        return z * 4 + lax.rem(x + step, 4)
-
-    def near_z(step):
-        return lax.rem(z + step, 4) * 4 + x
-
-    for step in range(1, 4):
-        for device in (near_x(step), near_z(step)):
-            pl.semaphore_signal(
-                barrier, inc=1, device_id=(device, head), device_id_type=MESH
-            )
     pl.semaphore_wait(barrier, 13)
 
     value_copies = []
@@ -743,7 +745,8 @@
     normed_copies[3].wait_recv()
     for quarter in range(4):
         own_sum[:, quarter * TILE : (quarter + 1) * TILE] = product(3, 4, quarter)
-    for quarter in range(4):
+    result_copies = []
+    for quarter in (2, 0, 3, 1):
         for place in range(2):
             copy(
                 partial_recv.at[place, quarter],
@@ -753,11 +756,19 @@
                 up,
             ).wait_recv()
         columns = slice(quarter * TILE, (quarter + 1) * TILE)
-        result[:, columns] = (
+        rounded[:, columns] = (
             own_sum[:, columns]
             + partial_recv[0, quarter].astype(F32)
             + partial_recv[1, quarter].astype(F32)
         ).astype(BF16)
+        result_copies.append(
+            pltpu.make_async_copy(
+                rounded.at[:, columns], result.at[:, columns], local_sem.at[quarter]
+            )
+        )
+        result_copies[-1].start()
+    for item in result_copies:
+        item.wait()
 
     for item in (
         value_copies
@@ -793,7 +804,7 @@
         kernel,
         out_shape=jax.ShapeDtypeStruct((CHUNK, OUTS), BF16),
         in_specs=[anywhere] * 9,
-        out_specs=pl.BlockSpec(memory_space=pltpu.VMEM),
+        out_specs=anywhere,
         scratch_shapes=[
             pltpu.VMEM((4, 2 * CHUNK, FEATS), BF16),
             pltpu.VMEM((CHUNKS * CHUNK, STATE), BF16),
@@ -823,6 +834,7 @@
             pltpu.VMEM((4, CHUNK, FEATS), BF16),
             pltpu.VMEM((4, CHUNK, 2 * FEATS), BF16),
             pltpu.VMEM((CHUNK, OUTS), F32),
+            pltpu.VMEM((CHUNK, OUTS), BF16),
             pltpu.VMEM((4, CHUNK, TILE), F32),
             pltpu.VMEM((3, 4, CHUNK, TILE), BF16),
             pltpu.VMEM((4, CHUNK, TILE), BF16),

time: 70.7 us -> 70.3 us (level)
  no operation moved by 1% of the time
where the time goes in v4:
time: 70.3 us; the launch traced here: 70.2 us
  Pallas kernels  68.2 us (97%)
  local copies, waits for them, and re-layouts  1.97 us (3%)
    pallas_call x1, Pallas kernels, on_device(): pl.pallas_call(kernel, out_shape=jax.ShapeDtypeStruct((CHUNK, OUTS), BF16...  68.2 us
    unnamed x1, local copies, waits for them, and re-layouts  1.97 us

profile of v4, /device:TPU:1, one launch (start us, length us, event | category | flops | bytes accessed | tf_op | source)
XLA Modules:
  0.0 70.2 jit_solution(14102525961798234075)
XLA Ops:
  0.0 68.2 %layer.1 = bf16[128,2560]{1,0:T(8,128)(2,1)} custom-call(bf16[128,5120]{1,0:T(8,128)(2,1)} %values.1, bf16[1024,128]{1,0:T(8,128)(2,1)} %state_in.1, bf16[1024,128]{1,0:T(8,128)(2,1)} %state_out.1, f32[10,1024]{1,0:T(8,128)} %bitcast.9, s32[8,128]{1,0:T(8,128)} %bitcast.10, f32[9,10,32]{2,1,0:T(8,128)} %bitcast.8, f32[1,10]{1,0:T(1,128)} %bitcast.11, ...), custom_call_target="tpu_custom_call" | custom-call | tf_op jit(solution)/shard_map/layer/pallas_call | solution.py:803
  68.2 2.0 %copy.11 = bf16[128,2560]{1,0:T(8,128)(2,1)} copy(bf16[128,2560]{1,0:T(8,128)(2,1)} %layer.1) | data formatting | bytes 1310720

commit v5 on v4

--- a/solution.py
+++ b/solution.py
@@ -91,7 +91,6 @@
     normed_send,
     normed_all,
     own_sum,
-    rounded,
     held,
     partial_send,
     relay_recv,
@@ -745,8 +744,7 @@
     normed_copies[3].wait_recv()
     for quarter in range(4):
         own_sum[:, quarter * TILE : (quarter + 1) * TILE] = product(3, 4, quarter)
-    result_copies = []
-    for quarter in (2, 0, 3, 1):
+    for quarter in range(4):
         for place in range(2):
             copy(
                 partial_recv.at[place, quarter],
@@ -756,19 +754,11 @@
                 up,
             ).wait_recv()
         columns = slice(quarter * TILE, (quarter + 1) * TILE)
-        rounded[:, columns] = (
+        result[:, columns] = (
             own_sum[:, columns]
             + partial_recv[0, quarter].astype(F32)
             + partial_recv[1, quarter].astype(F32)
         ).astype(BF16)
-        result_copies.append(
-            pltpu.make_async_copy(
-                rounded.at[:, columns], result.at[:, columns], local_sem.at[quarter]
-            )
-        )
-        result_copies[-1].start()
-    for item in result_copies:
-        item.wait()
 
     for item in (
         value_copies
@@ -804,7 +794,7 @@
         kernel,
         out_shape=jax.ShapeDtypeStruct((CHUNK, OUTS), BF16),
         in_specs=[anywhere] * 9,
-        out_specs=anywhere,
+        out_specs=pl.BlockSpec(memory_space=pltpu.VMEM),
         scratch_shapes=[
             pltpu.VMEM((4, 2 * CHUNK, FEATS), BF16),
             pltpu.VMEM((CHUNKS * CHUNK, STATE), BF16),
@@ -834,7 +824,6 @@
             pltpu.VMEM((4, CHUNK, FEATS), BF16),
             pltpu.VMEM((4, CHUNK, 2 * FEATS), BF16),
             pltpu.VMEM((CHUNK, OUTS), F32),
-            pltpu.VMEM((CHUNK, OUTS), BF16),
             pltpu.VMEM((4, CHUNK, TILE), F32),
             pltpu.VMEM((3, 4, CHUNK, TILE), BF16),
             pltpu.VMEM((4, CHUNK, TILE), BF16),

time: 70.3 us -> 70.6 us (level)
  no operation moved by 1% of the time
where the time goes in v5:
time: 70.6 us; the launch traced here: 70.4 us
  Pallas kernels  68.5 us (97%)
  local copies, waits for them, and re-layouts  1.97 us (3%)
    pallas_call x1, Pallas kernels, on_device(): pl.pallas_call(kernel, out_shape=jax.ShapeDtypeStruct((CHUNK, OUTS), BF16...  68.5 us
    unnamed x1, local copies, waits for them, and re-layouts  1.97 us

profile of v5, /device:TPU:1, one launch (start us, length us, event | category | flops | bytes accessed | tf_op | source)
XLA Modules:
  0.0 70.4 jit_solution(3530007090622543018)
XLA Ops:
  0.0 68.5 %layer.1 = bf16[128,2560]{1,0:T(8,128)(2,1)} custom-call(bf16[128,5120]{1,0:T(8,128)(2,1)} %values.1, bf16[1024,128]{1,0:T(8,128)(2,1)} %state_in.1, bf16[1024,128]{1,0:T(8,128)(2,1)} %state_out.1, f32[10,1024]{1,0:T(8,128)} %bitcast.9, s32[8,128]{1,0:T(8,128)} %bitcast.10, f32[9,10,32]{2,1,0:T(8,128)} %bitcast.8, f32[1,10]{1,0:T(1,128)} %bitcast.11, ...), custom_call_target="tpu_custom_call" | custom-call | tf_op jit(solution)/shard_map/layer/pallas_call | solution.py:793
  68.5 2.0 %copy.11 = bf16[128,2560]{1,0:T(8,128)(2,1)} copy(bf16[128,2560]{1,0:T(8,128)(2,1)} %layer.1) | data formatting | bytes 1310720
